TPU v7x, 256 devices: a whole 4x4x8 slice. The times are simulated.
256 devices in a mesh: lat: 4 (over x), lon: 2 (over core), ens: 32 (over z, y).
Axes of the slice: x: 4, y: 4, z: 8, core: 2. Of those that a mesh axis runs over, the one named last changes fastest.
Arguments:
- inputs: bfloat16 [32, 8, 1440, 256], P('ens', 'lat', 'lon'), may hold values from -12 to 12
- weight: bfloat16 [9, 256, 256], replicated, may hold values from -0.125 to 0.125
- spread: int32 [8], P('lat'), may hold values from 2 to 16, as said below
- target: bfloat16 [8, 1440, 256], P('lat', 'lon'), may hold values from -6 to 6
Outputs:
- response: bfloat16 [32, 8, 1440, 256], P('ens', 'lat', 'lon')
- grad_input: bfloat16 [32, 8, 1440, 256], P('ens', 'lat', 'lon')
- grad_weight: float32 [9, 256, 256], replicated
- loss: float32 [], replicated
Inputs may be any that keep to these rules, and one draw needn't show every extreme that they name: The filter of row o spans 2 spread[o] + 1 longitudes; spread is 16 on the 2 polar rows at each pole, which ignore it, and on the next row toward the equator.
All inputs are finite; a program needn't handle non-finite values.
Results may differ from a plain program's by a relative error of at most 0.009.
Values may be sent and summed in bfloat16 or wider, within the bound.
No kernel may reach another device: no remote copies, remote signals or barrier semaphores. Data moves between devices by JAX's collectives and lax.ppermute only.
A program may use at most 128 MiB of HBM per device.

v0:
```python
import math

import jax
import jax.numpy as jnp
from jax import lax
from jax.sharding import PartitionSpec as P

PCAP = 2
HMAX = 16


highest = lax.Precision.HIGHEST


def extended_2(block, sides, width):
    for axis, dim in sides:
        count = lax.axis_size(axis)
        forward = [(i, i + 1) for i in range(count - 1)]
        backward = [(target, source) for source, target in forward]
        low = lax.ppermute(
            lax.slice_in_dim(block, block.shape[dim] - width, None, axis=dim), axis, forward
        )
        high = lax.ppermute(lax.slice_in_dim(block, 0, width, axis=dim), axis, backward)
        block = jnp.concatenate([low, block, high], axis=dim)
    return block


def kernel_rows(spread_rows, lon_count, reach):
    halves = spread_rows.astype(jnp.float32)[:, None, None, None] / 2.0
    columns = jnp.arange(lon_count)
    window_cols = jnp.arange(lon_count + 2 * reach)
    offsets = (window_cols[None, :] - reach - columns[:, None]).astype(jnp.float32)
    centres = (jnp.arange(3) - 1).astype(jnp.float32)[None, :, None, None] * halves
    values = jnp.maximum(0.0, 1.0 - jnp.abs(offsets[None, None] - centres) / halves) / halves
    return values.astype(jnp.bfloat16)


def circle_basis(first_col, lon_count, circle):
    angles = 2.0 * math.pi * (first_col + jnp.arange(lon_count)).astype(jnp.float32) / circle
    return jnp.stack([jnp.ones_like(angles), jnp.cos(angles), jnp.sin(angles)])


def circular(circle_sums, basis, circle, row_count):
    cos_wave = basis[1][None, None, :, None]
    sin_wave = basis[2][None, None, :, None]
    pieces = []
    for lat_tap in range(3):
        tap_sums = circle_sums[:, :, lat_tap : lat_tap + row_count]
        mean_part = tap_sums[:, 0][:, :, None, :] / circle
        cosine_part = (
            2.0
            / circle
            * (cos_wave * tap_sums[:, 1][:, :, None, :] + sin_wave * tap_sums[:, 2][:, :, None, :])
        )
        sine_part = (
            2.0
            / circle
            * (cos_wave * tap_sums[:, 2][:, :, None, :] - sin_wave * tap_sums[:, 1][:, :, None, :])
        )
        pieces += [jnp.broadcast_to(mean_part, cosine_part.shape), cosine_part, sine_part]
    return jnp.stack(pieces, 2)


def crps_terms(values, every_member, truth, lat_weight, member_total):
    miss = values - truth
    own_dist = jnp.sqrt(miss * miss + 0.25)
    own_slope = miss / own_dist

    def add_member(member, carry):
        pair_dist, pair_slope = carry
        other = lax.dynamic_index_in_dim(every_member, member, 0, keepdims=True).astype(jnp.float32)
        gap_value = values - other
        distance = jnp.sqrt(gap_value * gap_value + 0.25)
        return (pair_dist + distance, pair_slope + gap_value / distance)

    start = (jnp.zeros_like(values), jnp.zeros_like(values))
    pair_dist, pair_slope = lax.fori_loop(0, member_total, add_member, start)
    pair_dist = pair_dist - 0.5
    scores = own_dist / member_total - pair_dist / (2 * member_total * (member_total - 1))
    weighted = jnp.sum(lat_weight * scores)
    slopes = (
        lat_weight * (own_slope / member_total - pair_slope / (member_total * (member_total - 1)))
    ).astype(jnp.bfloat16)
    return (weighted, slopes)


def per_device(inputs, weight, spread, target):
    ens_local, row_count, lon_count, channels = inputs.shape
    reach = HMAX
    lat_total = row_count * lax.axis_size("lat")
    lon_total = lon_count * lax.axis_size("lon")
    lon_first = lax.axis_index("lon") * lon_count
    global_rows = lax.axis_index("lat") * row_count + jnp.arange(row_count)
    polar_rows = (global_rows < PCAP) | (global_rows >= lat_total - PCAP)
    polar_mask = polar_rows[None, :, None, None, None]
    kernels = kernel_rows(spread, lon_count, reach)
    local_basis = circle_basis(lon_first, lon_count, lon_total)
    extended = extended_2(inputs, (("lat", 1),), 1)
    whole_circle = lax.all_gather(extended, "lon", axis=2, tiled=True)
    window_start = (lon_first - reach + lon_total) % lon_total
    doubled = jnp.concatenate([whole_circle, whole_circle], 2)
    window = lax.dynamic_slice_in_dim(doubled, window_start, lon_count + 2 * reach, 2)
    full_basis = circle_basis(0, lon_total, lon_total)
    circle_sums = jnp.einsum(
        "pj,erjc->eprc", full_basis, whole_circle.astype(jnp.float32), precision=highest
    )
    banded = jnp.concatenate(
        [
            jnp.einsum(
                "objq,eoqc->eobjc",
                kernels,
                window[:, lat_tap : lat_tap + row_count],
                preferred_element_type=jnp.float32,
            )
            for lat_tap in range(3)
        ],
        2,
    )
    rounds = circular(circle_sums, local_basis, lon_total, row_count)
    features = jnp.where(polar_mask, rounds, banded).astype(jnp.bfloat16)
    response = jnp.einsum(
        "eokjc,kcd->eojd", features, weight, preferred_element_type=jnp.float32
    ).astype(jnp.bfloat16)
    member_total = ens_local * lax.axis_size("ens")
    row_weight = jnp.sin(math.pi * (global_rows.astype(jnp.float32) + 0.5) / lat_total)
    ensemble = lax.all_gather(response, "ens", axis=0, tiled=True)
    truth = target.astype(jnp.float32)[None]
    weighted, slopes = crps_terms(
        response.astype(jnp.float32), ensemble, truth, row_weight[None, :, None, None], member_total
    )
    loss_part = weighted / (lat_total * lon_total * channels)
    weight_part = jnp.einsum(
        "eokjc,eojd->kcd", features, slopes, preferred_element_type=jnp.float32
    )
    weight_sum, loss = lax.psum((weight_part, loss_part), ("lat", "lon", "ens"))
    grad_weight = weight_sum * math.sqrt(weight.shape[0] * channels) / (lat_total * lon_total)
    feature_grad = jnp.einsum(
        "eojd,kcd->eokjc", slopes, weight, preferred_element_type=jnp.float32
    ).astype(jnp.bfloat16)
    zero_grad = jnp.zeros_like(feature_grad)
    band_grad = jnp.where(polar_mask, zero_grad, feature_grad)
    circle_grad = jnp.where(polar_mask, feature_grad, zero_grad)
    window_grad = jnp.zeros(
        (ens_local, row_count + 2, lon_count + 2 * reach, channels), jnp.float32
    )
    sum_grad = jnp.zeros((ens_local, 3, row_count + 2, channels), jnp.float32)
    cos_wave = local_basis[1]
    sin_wave = local_basis[2]
    for lat_tap in range(3):
        picked = band_grad[:, :, 3 * lat_tap : 3 * lat_tap + 3]
        window_grad = window_grad.at[:, lat_tap : lat_tap + row_count].add(
            jnp.einsum("objq,eobjc->eoqc", kernels, picked, preferred_element_type=jnp.float32)
        )
        tap_grad = circle_grad[:, :, 3 * lat_tap : 3 * lat_tap + 3].astype(jnp.float32)
        mean_grad = jnp.sum(tap_grad[:, :, 0], axis=2) / lon_total
        cos_grad = (
            2.0
            / lon_total
            * (
                jnp.einsum("j,eojc->eoc", cos_wave, tap_grad[:, :, 1], precision=highest)
                - jnp.einsum("j,eojc->eoc", sin_wave, tap_grad[:, :, 2], precision=highest)
            )
        )
        sin_grad = (
            2.0
            / lon_total
            * (
                jnp.einsum("j,eojc->eoc", sin_wave, tap_grad[:, :, 1], precision=highest)
                + jnp.einsum("j,eojc->eoc", cos_wave, tap_grad[:, :, 2], precision=highest)
            )
        )
        sum_grad = sum_grad.at[:, :, lat_tap : lat_tap + row_count].add(
            jnp.stack([mean_grad, cos_grad, sin_grad], 1)
        )
    spread_back = jnp.einsum("pj,eprc->erjc", full_basis, sum_grad, precision=highest)
    placed = jnp.zeros((ens_local, row_count + 2, 2 * lon_total, channels), jnp.float32)
    placed = lax.dynamic_update_slice_in_dim(placed, window_grad, window_start, 2)
    spread_back = spread_back + placed[:, :, :lon_total] + placed[:, :, lon_total:]
    core = lax.psum_scatter(
        spread_back.astype(jnp.bfloat16), "lon", scatter_dimension=2, tiled=True
    ).astype(jnp.float32)
    edges = jnp.concatenate([core[:, :1], core[:, row_count + 1 :]], 1)
    arrived_rows = extended_2(edges.astype(jnp.bfloat16), (("lat", 1),), 1).astype(edges.dtype)
    inner = core[:, 1 : row_count + 1]
    inner = inner.at[:, 0].add(arrived_rows[:, 0])
    inner = inner.at[:, row_count - 1].add(arrived_rows[:, 3])
    return (response, inner.astype(jnp.bfloat16), grad_weight, loss)


def solution(mesh):
    in_specs = (P("ens", "lat", "lon", None), P(), P("lat"), P("lat", "lon", None))
    out_specs = (P("ens", "lat", "lon", None), P("ens", "lat", "lon", None), P(), P())
    return jax.shard_map(
        per_device, mesh=mesh, in_specs=in_specs, out_specs=out_specs, check_vma=False
    )
```

profile of v0, /device:TPU:2, one launch (start us, length us, event | category | flops | bytes accessed | tf_op | source)
XLA Modules:
  0.0 740.7 jit_solution(5865980801284775677)
XLA Ops:
  7.2 1.2 fusion.72
  8.5 3.4 collective-permute-start
  11.9 2.5 collective-permute-start.1
  14.4 6.3 collective-permute-done
  20.7 3.1 collective-permute-done.1
  23.8 2.4 pad_maximum_fusion
  27.0 19.3 %all-gather.4.cloned.1.call-done = bf16[1,4,1440,256]{3,2,1,0:T(8,128)(2,1)} async-done(((bf16[1,4,720,256]{3,2,1,0:T(8,128)(2,1)}), bf16[1,4,1440,256]{3,2,1,0:T(8,128)(2,1)}) %all-gather.4.cloned.1.call-update) | async-done | bytes 2949136 | tf_op jit(solution)/shard_map/all_gather | solution.py:99
  46.2 3.3 fusion.19
  49.6 1.8 fusion.9
  51.4 3.2 convolution_bitcast_fusion.1
  54.6 3.2 convolution_bitcast_fusion
  57.9 3.2 convolution_bitcast_fusion.2
  64.3 2.8 copy-done.4
  67.1 2.8 bitcast_convert_fusion
  71.5 174.4 %all-gather.6.cloned.1.call-done = bf16[64,720,256]{2,1,0:T(8,128)(2,1)} async-done(((bf16[2,720,256]{2,1,0:T(8,128)(2,1)}), bf16[64,720,256]{2,1,0:T(8,128)(2,1)}) %all-gather.6.cloned.1.call-update) | async-done | bytes 23592976 | tf_op jit(solution)/shard_map/all_gather | solution.py:126
  245.9 140.6 %while.24 = (s32[]{:T(128)}, f32[1,2,720,256]{3,2,1,0:T(8,128)}, f32[1,2,720,256]{3,2,1,0:T(8,128)}, bf16[32,2,720,256]{3,2,1,0:T(8,128)(2,1)}, f32[1,2,720,256]{3,2,1,0:T(8,128)S(1)}, /*index=5*/s32[]{:T(128)}, s32[]{:T(128)}) while((s32[]{:T(128)}, f32[1,2,720,256]{3,2,1,0:T(8,128)}, f32[1,2,720,256]{3,2,1,0:T(8,128)}, ...), condition=%wide.region_1.2_spmd.clone, body=%wide.region_0.1_spmd.clone.sunk | while | flops 3317763 | bytes 8110179 | solution.py:77
  245.9 3.6 select_add_fusion.3
  249.5 4.4 select_add_fusion.3
  253.9 4.4 select_add_fusion.3
  258.3 4.4 select_add_fusion.3
  262.7 4.4 select_add_fusion.3
  267.2 4.4 select_add_fusion.3
  271.6 4.4 select_add_fusion.3
  276.0 4.4 select_add_fusion.3
  280.4 4.4 select_add_fusion.3
  284.8 4.4 select_add_fusion.3
  289.3 4.4 select_add_fusion.3
  293.7 4.4 select_add_fusion.3
  298.1 4.4 select_add_fusion.3
  302.5 4.4 select_add_fusion.3
  306.9 4.4 select_add_fusion.3
  311.4 4.4 select_add_fusion.3
  315.8 4.4 select_add_fusion.3
  320.2 4.4 select_add_fusion.3
  324.6 4.4 select_add_fusion.3
  329.0 4.4 select_add_fusion.3
  333.5 4.4 select_add_fusion.3
  337.9 4.4 select_add_fusion.3
  342.3 4.4 select_add_fusion.3
  346.7 4.4 select_add_fusion.3
  351.2 4.4 select_add_fusion.3
  355.6 4.4 select_add_fusion.3
  360.0 4.4 select_add_fusion.3
  364.4 4.4 select_add_fusion.3
  368.8 4.4 select_add_fusion.3
  373.3 4.4 select_add_fusion.3
  377.7 4.4 select_add_fusion.3
  382.1 4.4 select_add_fusion.3
  386.5 3.9 fusion.14
  390.4 3.9 fusion.1
  399.8 5.7 fusion.12
  405.5 1.8 scatter-add.31
  407.4 6.8 fusion.11
  414.2 6.8 fusion.10
  420.9 5.4 broadcast_in_dim.38
  426.3 8.8 %dynamic_update_slice.3 = f32[1,4,2880,256]{3,2,1,0:T(8,128)} dynamic-update-slice(f32[1,4,2880,256]{3,2,1,0:T(8,128)} %broadcast_in_dim.38, f32[1,4,752,256]{3,2,1,0:T(8,128)} %fusion.10, s32[]{:T(128)} %constant.322.clone.1, s32[]{:T(128)} %constant.322.clone.1, s32[]{:T(128)S(6)} %select_n.39, s32[]{:T(128)} %constant.322.clone.1) | dynamic-update-slice | bytes 6160388 | tf_op jit(solution)/shard_map/dynamic_update_slice | solution.py:177
  435.2 9.4 %fusion.3 = bf16[1,4,1440,256]{3,2,1,0:T(8,128)(2,1)} fusion(f32[1,4,2880,256]{3,2,1,0:T(8,128)} %dynamic_update_slice.3, f32[3,4,256]{2,0,1:T(4,128)S(1)} %fusion.41, f32[1,1440]{1,0:T(1,128)S(1)} %copy-done.11, f32[1,1440]{1,0:T(1,128)S(1)} %copy-done.13, f32[3]{0:T(128)S(1)} %copy-done.15), kind=kOutput, calls=%fused_computation.12 | convolution fusion | flops 57516480 | bytes 14769420 | tf_op jit(solution)/shard_map/pj,eprc->erjc/dot_general | solution.py:175
  445.7 6.4 convolution_bitcast_fusion.3
  452.8 73.8 %psum.15 = f32[]{:T(128)} all-reduce(f32[]{:T(128)S(6)} %div.141), channel_id=1, replica_groups=mesh['lat'=4,'lon'=2,'ens'=32] {'lat','lon','ens'}, use_global_device_ids=true, to_apply=%region_8.9 | all-reduce | flops 1 | bytes 8 | tf_op jit(solution)/shard_map/psum | solution.py:135
  526.6 1.3 fusion.71
  527.9 2.9 collective-permute-start.2
  530.8 2.9 collective-permute-start.3
  533.8 195.4 %all-reduce.4.cloned.1.call-done = f32[9,256,256]{2,1,0:T(8,128)} async-done(((f32[9,256,256]{2,1,0:T(8,128)}), f32[9,256,256]{2,1,0:T(8,128)}) %all-reduce.4.cloned.1.call-update) | async-done | bytes 2359312 | tf_op jit(solution)/shard_map/psum | solution.py:135
  729.1 3.3 broadcast_multiply_fusion
  (117 shorter events, 13.5 us)
Async XLA Ops:
  7.2 60.0 %copy-start = (bf16[9,256,256]{2,1,0:T(8,128)(2,1)S(1)}, bf16[9,256,256]{2,1,0:T(8,128)(2,1)}, u32[]{:S(2)}) copy-start(bf16[9,256,256]{2,1,0:T(8,128)(2,1)} %param.23) | copy-start | bytes 3538948
  7.2 19.3 %copy-start.16 = (s32[2]{0:T(128)S(1)}, s32[2]{0:T(128)}, u32[]{:S(2)}) copy-start(s32[2]{0:T(128)} %param.24) | copy-start | bytes 28
  7.2 39.1 %all-gather.4.cloned.1.call-start = ((), (), s32[]{:S(2)}) async-start(), calls=%async_computation.1 | async-start | bytes 4423680 | tf_op jit(solution)/shard_map/all_gather | solution.py:99
  8.5 12.2 %collective-permute-start = (bf16[1,1,720,256]{3,2,1,0:T(8,128)(2,1)S(1)}, bf16[1,1,720,256]{3,2,1,0:T(8,128)(2,1)S(1)}, u32[]{:S(2)}, u32[]{:S(2)}) collective-permute-start(bf16[1,1,720,256]{3,2,1,0:T(8,128)(2,1)S(1)} %get-tuple-element.236), channel_id=1, source_target_pairs={{0,64},{64,128},{128,192},{1,65},{65,129},{129,193},{2,66},{66,130... | collective-permute-start | bytes 1105928 | tf_op jit(solution)/shard_map/ppermute | solution.py:20
  11.9 11.9 %collective-permute-start.1 = (bf16[1,1,720,256]{3,2,1,0:T(8,128)(2,1)S(1)}, bf16[1,1,720,256]{3,2,1,0:T(8,128)(2,1)S(1)}, u32[]{:S(2)}, u32[]{:S(2)}) collective-permute-start(bf16[1,1,720,256]{3,2,1,0:T(8,128)(2,1)S(1)} %get-tuple-element.237), channel_id=1, source_target_pairs={{64,0},{128,64},{192,128},{65,1},{129,65},{193,129},{66,2},{130,66... | collective-permute-start | bytes 1105928 | tf_op jit(solution)/shard_map/ppermute | solution.py:23
  26.3 219.6 %all-gather.6.cloned.1.call-start = ((), (), s32[]{:S(2)}) async-start(), calls=%async_computation.4 | async-start | bytes 24330240 | tf_op jit(solution)/shard_map/all_gather | solution.py:126
  26.4 25.0 %copy-start.14 = (f32[3]{0:T(128)}, f32[3]{0:T(128)S(1)}, u32[]{:S(2)}) copy-start(f32[3]{0:T(128)S(1)} %pad.37.clone) | copy-start | bytes 40
  26.7 24.6 %copy-start.10 = (f32[1,1440]{1,0:T(1,128)}, f32[1,1440]{1,0:T(1,128)S(1)}, u32[]{:S(2)}) copy-start(f32[1,1440]{1,0:T(1,128)S(1)} %get-tuple-element.247) | copy-start | bytes 17284
  26.7 24.6 %copy-start.12 = (f32[1,1440]{1,0:T(1,128)}, f32[1,1440]{1,0:T(1,128)S(1)}, u32[]{:S(2)}) copy-start(f32[1,1440]{1,0:T(1,128)S(1)} %get-tuple-element.248) | copy-start | bytes 17284
  27.0 30.9 %copy-start.6 = (f32[720,752]{1,0:T(8,128)}, f32[720,752]{1,0:T(8,128)S(1)}, u32[]{:S(2)}) copy-start(f32[720,752]{1,0:T(8,128)S(1)} %subtract_convert_fusion) | copy-start | bytes 6497284
  46.2 3.3 copy-start.2
  64.3 2.8 copy-start.4
  69.9 456.7 %reduce-scatter.2.cloned.1.call-start = ((), (), s32[]{:S(2)}) async-start(), calls=%async_computation.2 | async-start | bytes 4423680 | tf_op jit(solution)/shard_map/reduce_scatter | solution.py:179
  245.9 140.6 %copy-start.5 = (bf16[2,720,256]{2,1,0:T(8,128)(2,1)S(1)}, bf16[2,720,256]{2,1,0:T(8,128)(2,1)}, u32[]{:S(2)}) copy-start(bf16[2,720,256]{2,1,0:T(8,128)(2,1)} %bitcast_convert_fusion) | copy-start | bytes 2211844
  390.4 3.9 copy-start.8
  397.1 2.7 copy-start.7
  426.3 8.8 %copy-start.11 = (f32[1,1440]{1,0:T(1,128)S(1)}, f32[1,1440]{1,0:T(1,128)}, u32[]{:S(2)}) copy-start(f32[1,1440]{1,0:T(1,128)} %copy-done.10) | copy-start | bytes 17284
  426.3 8.8 %copy-start.13 = (f32[1,1440]{1,0:T(1,128)S(1)}, f32[1,1440]{1,0:T(1,128)}, u32[]{:S(2)}) copy-start(f32[1,1440]{1,0:T(1,128)} %copy-done.12) | copy-start | bytes 17284
  426.3 8.8 %copy-start.15 = (f32[3]{0:T(128)S(1)}, f32[3]{0:T(128)}, u32[]{:S(2)}) copy-start(f32[3]{0:T(128)} %copy-done.14) | copy-start | bytes 40
  444.6 1.1 copy-start.9
  444.6 284.5 %all-reduce.4.cloned.1.call-start = ((), (), s32[]{:S(2)}) async-start(), calls=%async_computation.3 | async-start | bytes 4718592 | tf_op jit(solution)/shard_map/psum | solution.py:135
  526.6 205.8 %copy-start.3 = (bf16[1,4,720,256]{3,2,1,0:T(8,128)(2,1)S(1)}, bf16[1,4,720,256]{3,2,1,0:T(8,128)(2,1)}, u32[]{:S(2)}) copy-start(bf16[1,4,720,256]{3,2,1,0:T(8,128)(2,1)} %reduce-scatter.2.cloned.1.call-done) | copy-start | bytes 4423684
  527.9 205.0 %collective-permute-start.2 = (bf16[1,1,720,256]{3,2,1,0:T(8,128)(2,1)S(1)}, bf16[1,1,720,256]{3,2,1,0:T(8,128)(2,1)S(1)}, u32[]{:S(2)}, u32[]{:S(2)}) collective-permute-start(bf16[1,1,720,256]{3,2,1,0:T(8,128)(2,1)S(1)} %get-tuple-element.234), channel_id=1, source_target_pairs={{0,64},{64,128},{128,192},{1,65},{65,129},{129,193},{2,66},{66,130... | collective-permute-start | bytes 1105928 | tf_op jit(solution)/shard_map/ppermute | solution.py:20
  530.8 202.0 %collective-permute-start.3 = (bf16[1,1,720,256]{3,2,1,0:T(8,128)(2,1)S(1)}, bf16[1,1,720,256]{3,2,1,0:T(8,128)(2,1)S(1)}, u32[]{:S(2)}, u32[]{:S(2)}) collective-permute-start(bf16[1,1,720,256]{3,2,1,0:T(8,128)(2,1)S(1)} %get-tuple-element.235), channel_id=1, source_target_pairs={{64,0},{128,64},{192,128},{65,1},{129,65},{193,129},{66,2},{130,66... | collective-permute-start | bytes 1105928 | tf_op jit(solution)/shard_map/ppermute | solution.py:23
  732.9 1.3 copy-start.1
Sparse Core Ops, SparseCore 0:
  26.4 19.8 all-gather.3
  70.1 175.7 all-gather.5
  444.7 13.3 reduce-scatter.1
  464.0 265.1 all-reduce.3
where the time goes:
time: 742 us; the launch traced here: 741 us
  waiting for transfers between devices  399 us (54%)
  other arithmetic  159 us (21%)
  blocking collectives  73.8 us (10%)
  matrix products  59.5 us (8%)
  local copies, waits for them, and re-layouts  23.1 us (3%)
  between operations  15.1 us (2%)
  starting transfers between devices  12.1 us (2%)
    psum x1, waiting for transfers between devices, per_device(): weight_sum, loss = lax.psum((weight_part, loss_part), ('lat', 'lon', 'ens'))  195 us
    all_gather x1, waiting for transfers between devices, per_device(): ensemble = lax.all_gather(response, 'ens', axis=0, tiled=True)  174 us
    add x32, other arithmetic, add_member(): return (pair_dist + distance, pair_slope + gap_value / distance)  141 us
    psum x1, blocking collectives, per_device(): weight_sum, loss = lax.psum((weight_part, loss_part), ('lat', 'lon', 'ens'))  73.8 us
    all_gather x1, waiting for transfers between devices, per_device(): whole_circle = lax.all_gather(extended, 'lon', axis=2, tiled=True)  19.3 us
    dot_general x3, matrix products, per_device(): jnp.einsum('objq,eobjc->eoqc', kernels, picked, preferred_element_type=jn...  19.3 us
  transfers between devices with their start and end apart: 8, of which 5 were waited for; matrix products, arithmetic and copies ran while one was open for 2% of the time, Pallas kernels for 0%

commit v1 on v0

v1 whole, which is shorter than its diff:
```python
import functools
import math

import jax
import jax.numpy as jnp
import numpy as np
from jax import lax
from jax.experimental import pallas as pl
from jax.experimental.pallas import tpu as pltpu
from jax.sharding import PartitionSpec as P

PCAP = 2
HMAX = 16
BLK = 224
VMEM_LIMIT = 24 << 20
F32 = jnp.float32
BF16 = jnp.bfloat16


def split(values):
    high = lax.reduce_precision(values, 8, 7)
    return high.astype(BF16), (values - high).astype(BF16)


def dot(a, b, ca, cb):
    return lax.dot_general(a, b, (((ca,), (cb,)), ((), ())), preferred_element_type=F32)


def circle_waves(lon_index, lon_count, lon_total):
    angles = 2.0 * np.pi * np.arange(lon_total) / lon_total
    both = np.stack([np.cos(angles), np.sin(angles)])
    high = both.astype(BF16)
    low = (both - high.astype(np.float64)).astype(BF16)
    basis = np.concatenate([high, np.ones_like(high[:1]), low])
    columns = both.T.astype(np.float32).reshape(-1, lon_count, 2)
    basis = basis.reshape(5, -1, lon_count).transpose(1, 0, 2)
    pick = functools.partial(lax.dynamic_index_in_dim, index=lon_index, axis=0, keepdims=False)
    return pick(jnp.asarray(columns)), pick(jnp.asarray(basis))


def blocks(width):
    return [(start, min(BLK, width - start)) for start in range(0, width, BLK)]


def band_blocks(spread_rows, band_flags, reach):
    wide = spread_rows.astype(F32)[:, None, None, None]
    halves = jnp.where(wide > 0, wide, 2.0) / 2.0
    offsets = (jnp.arange(BLK + 2 * reach)[None, :] - reach - jnp.arange(BLK)[:, None]).astype(F32)
    centres = (jnp.arange(3) - 1).astype(F32)[None, :, None, None] * halves
    values = jnp.maximum(0.0, 1.0 - jnp.abs(offsets[None, None] - centres) / halves) / halves
    values = jnp.where(band_flags[:, None, None, None], values, 0.0)
    return values.astype(BF16)


def circle_parcel(rows, basis, reach):
    count, width, channels = rows.shape
    sums = jnp.einsum("pj,rjc->rpc", basis, rows, preferred_element_type=F32)
    sums = jnp.concatenate([sums[:, :2] + sums[:, 3:], sums[:, 2:3]], 1)
    high, low = split(sums)
    spare = jnp.zeros((count, reach - 6, channels), BF16)
    parcel = jnp.concatenate([rows[:, :reach], rows[:, width - reach :], high, low, spare], 1)
    return sums, lax.ppermute(parcel, "lon", [(0, 1), (1, 0)])


def extend_lon(rows, basis, spread_rows, reach):
    count, _, channels = rows.shape
    sums, other = circle_parcel(rows, basis, reach)
    total = sums + other[:, 2 * reach : 2 * reach + 3].astype(F32)
    total = total + other[:, 2 * reach + 3 : 2 * reach + 6].astype(F32)
    high, low = split(total)
    mark = jnp.broadcast_to(spread_rows.astype(BF16)[:, None, None], (count, reach - 6, channels))
    return jnp.concatenate(
        [other[:, reach : 2 * reach], rows, other[:, :reach], high, low, mark], 1
    )


def lat_neighbours(rows):
    count = lax.axis_size("lat")
    low = lax.ppermute(rows[-1:], "lat", [(i, i + 1) for i in range(count - 1)])
    high = lax.ppermute(rows[:1], "lat", [(i + 1, i) for i in range(count - 1)])
    return low, high


def convolved(row, pairs, weight_ref, band_ref, wave_ref, flag_ref):
    width = wave_ref.shape[0]
    circle = 2 * width
    reach = HMAX
    ext = width + 2 * reach
    extras = []
    total = [None] * len(blocks(width))
    for shape in range(3):
        mixed = None
        for source, tap in pairs:
            part = dot(source[...], weight_ref[3 * tap + shape], 1, 0)
            mixed = part if mixed is None else mixed + part
        extras.append(mixed[ext : ext + 3] + mixed[ext + 3 : ext + 6])
        mixed = mixed.astype(BF16)
        for part, (start, size) in enumerate(blocks(width)):
            piece = dot(
                band_ref[row, shape, :size, : size + 2 * reach],
                mixed[start : start + size + 2 * reach],
                1,
                0,
            )
            total[part] = piece if shape == 0 else total[part] + piece
    polar = flag_ref[row]
    flat = extras[0][2:3] * (polar / circle)
    with_cos = (extras[1][0:1] + extras[2][1:2]) * (polar * 2.0 / circle)
    with_sin = (extras[1][1:2] - extras[2][0:1]) * (polar * 2.0 / circle)
    answers = []
    for part, (start, size) in enumerate(blocks(width)):
        at = pl.ds(start, size)
        answers.append(
            total[part] + (flat + wave_ref[at, 0:1] * with_cos + wave_ref[at, 1:2] * with_sin)
        )
    return answers


def own_rows_kernel(own_ref, weight_ref, band_ref, wave_ref, flag_ref, out_ref):
    for row in range(2):
        pairs = [(own_ref.at[0], 1 - row), (own_ref.at[1], 2 - row)]
        parts = convolved(row, pairs, weight_ref, band_ref, wave_ref, flag_ref)
        for (start, size), part in zip(blocks(wave_ref.shape[0]), parts):
            out_ref[row, pl.ds(start, size)] = part


def outer_rows_kernel(
    low_ref, high_ref, begun_ref, weight_ref, band_ref, wave_ref, flag_ref, out_ref, sent_ref
):
    width = wave_ref.shape[0]
    for row, source, tap in ((0, low_ref, 0), (1, high_ref, 2)):
        parts = convolved(row, [(source.at[0], tap)], weight_ref, band_ref, wave_ref, flag_ref)
        for (start, size), part in zip(blocks(width), parts):
            answer = (begun_ref[row, pl.ds(start, size)] + part).astype(BF16)
            out_ref[row, pl.ds(start, size)] = answer
            sent_ref[pl.ds(row * width + start, size)] = answer
    spare = sent_ref.shape[0] - 2 * width
    sent_ref[2 * width :] = jnp.zeros((spare, sent_ref.shape[1]), BF16)


def spread_back_rows(ext_row, row, band_ref, wave_ref, polar):
    width = wave_ref.shape[0]
    circle = 2 * width
    reach = HMAX
    ext = width + 2 * reach
    sums = ext_row[ext : ext + 16, :].astype(F32)
    sums = (sums[0:3] + sums[3:6]) * polar
    cos_sum, sin_sum, flat = sums[0:1] * (2.0 / circle), sums[1:2] * (2.0 / circle), sums[2:3]
    flat = flat / circle
    answers = []
    for shape in range(3):
        pieces = []
        for start, size in blocks(width):
            piece = dot(
                band_ref[row, 2 - shape, :size, : size + 2 * reach],
                ext_row[pl.ds(start, size + 2 * reach), :],
                1,
                0,
            )
            at = pl.ds(start, size)
            cos_wave, sin_wave = wave_ref[at, 0:1], wave_ref[at, 1:2]
            if shape == 0:
                piece = piece + flat
            elif shape == 1:
                piece = piece + (cos_wave * cos_sum + sin_wave * sin_sum)
            else:
                piece = piece + (sin_wave * cos_sum - cos_wave * sin_sum)
            pieces.append(piece.astype(BF16))
        answers.append(jnp.concatenate(pieces, 0))
    return answers


def weight_grad_kernel(
    slope_ref,
    sums_ref,
    other_ref,
    low_ref,
    own_ref,
    high_ref,
    band_ref,
    wave_ref,
    flag_ref,
    lon_ref,
    spread_ref,
    mine_ref,
    theirs_ref,
    ext_ref,
    back_ref,
    field_ref,
    sems,
    *,
    scale,
):
    width = wave_ref.shape[0]
    reach = HMAX
    inner = pl.ds(reach, width)
    channels = low_ref.shape[-1]
    copies = [
        pltpu.make_async_copy(slope_ref.at[pl.ds(0, width)], ext_ref.at[0, inner], sems.at[0]),
        pltpu.make_async_copy(slope_ref.at[pl.ds(width, width)], ext_ref.at[1, inner], sems.at[1]),
        pltpu.make_async_copy(low_ref.at[0, inner], field_ref.at[0], sems.at[2]),
        pltpu.make_async_copy(own_ref.at[0, inner], field_ref.at[1], sems.at[3]),
        pltpu.make_async_copy(own_ref.at[1, inner], field_ref.at[2], sems.at[4]),
        pltpu.make_async_copy(high_ref.at[0, inner], field_ref.at[3], sems.at[5]),
    ]
    for copy in copies:
        copy.start()
    for row in range(2):
        total = sums_ref[row] + other_ref[row, 2 * reach : 2 * reach + 3].astype(F32)
        total = total + other_ref[row, 2 * reach + 3 : 2 * reach + 6].astype(F32)
        high = total.astype(BF16)
        low = (total - high.astype(F32)).astype(BF16)
        mark = jnp.full((reach - 6, channels), spread_ref[row], F32).astype(BF16)
        ext_ref[row, :reach] = other_ref[row, reach : 2 * reach]
        ext_ref[row, reach + width : 2 * reach + width] = other_ref[row, :reach]
        ext_ref[row, 2 * reach + width :] = jnp.concatenate([high, low, mark], 0)
    for row in range(2):
        copies[row].wait()
        backs = spread_back_rows(ext_ref.at[row], row, band_ref, wave_ref, flag_ref[row])
        for shape in range(3):
            back_ref[row, :, shape * channels : (shape + 1) * channels] = backs[shape]
    for copy in copies[2:]:
        copy.wait()
    half = mine_ref.shape[0] // 2
    lanes = channels // 2
    for tap in range(3):
        part = dot(field_ref[tap], back_ref[0], 0, 0)
        part = ((part + dot(field_ref[tap + 1], back_ref[1], 0, 0)) * scale).astype(BF16)
        for shape in range(3):
            first = (3 * tap + shape) * channels
            for start in range(0, channels, channels // 2):
                owner, at = divmod(first + start, half)
                for side in range(2):
                    left = shape * channels + side * lanes
                    piece = part[start : start + channels // 2, left : left + lanes]
                    into = pl.ds(side * half + at, channels // 2)

                    @pl.when(lon_ref[0] == owner)
                    def _():
                        mine_ref[into] = piece

                    @pl.when(lon_ref[0] != owner)
                    def _():
                        theirs_ref[into] = piece


def merge_kernel(mine_ref, theirs_ref, loss_ref, out_ref):
    count, rows, _ = out_ref.shape
    piece = mine_ref.shape[0] // count
    share = loss_ref[...]
    high = share.astype(BF16)
    low = (share - high.astype(F32)).astype(BF16)
    blank = jnp.zeros((rows - piece - 2, out_ref.shape[2]), BF16)
    mark = jnp.concatenate([high, low, blank], 0)
    for i in range(count):
        at = pl.ds(i * piece, piece)
        total = mine_ref[at].astype(F32) + theirs_ref[at].astype(F32)
        out_ref[i, :piece] = total.astype(BF16)
        out_ref[i, piece:] = mark


def whole_kernel(own_ref, other_ref, lon_ref, out_ref, loss_ref):
    count, _, lanes = own_ref.shape
    half = out_ref.shape[0] // 2
    side_count = count // 2
    piece = half // side_count
    for source, owner in ((own_ref, lon_ref[0]), (other_ref, 1 - lon_ref[0])):
        base = owner * half
        for i in range(count):
            side, at = divmod(i, side_count)
            into = pl.ds(pl.multiple_of(base + at * piece, 8), piece)
            out_ref[into, side * lanes : (side + 1) * lanes] = source[i, :piece].astype(F32)
    shares = own_ref[0, piece : piece + 2].astype(F32) + other_ref[0, piece : piece + 2].astype(F32)
    loss_ref[0, 0] = jnp.sum(shares)


def input_grad_kernel(
    low_ref, own_ref, high_ref, weight_ref, band_ref, wave_ref, flag_ref, out_ref, sum_ref
):
    rows = (low_ref.at[0], own_ref.at[0], own_ref.at[1], high_ref.at[0])
    for row in range(4):
        backs = spread_back_rows(rows[row], row, band_ref, wave_ref, flag_ref[row])
        for target in range(2):
            tap = target - row + 2
            if tap < 0 or tap > 2:
                continue
            part = dot(backs[0], weight_ref[3 * tap], 1, 1)
            for shape in (1, 2):
                part += dot(backs[shape], weight_ref[3 * tap + shape], 1, 1)
            if tap == 2:
                sum_ref[target] = part
            elif tap == 1:
                sum_ref[target] += part
            else:
                out_ref[target] = (sum_ref[target] + part).astype(BF16)


def crps_kernel(z_ref, truth_ref, weight_ref, slope_ref, loss_ref, value_ref, grad_ref):
    members, count, channels = z_ref.shape
    lat_weight = weight_ref[0]
    group = 8
    pair_scale = -1.0 / (members * (members - 1))
    value_ref[...] = z_ref[...].astype(F32)

    def tile(index, total):
        first = pl.multiple_of((index // (channels // 128)) * 8, 8)
        lane = pl.multiple_of((index % (channels // 128)) * 128, 128)
        at = (pl.ds(first, 8), pl.ds(lane, 128))
        truth = truth_ref[at].astype(F32)
        own = jnp.zeros((8, 128), F32)
        pair = jnp.zeros((8, 128), F32)
        moment = jnp.zeros((8, 128), F32)
        for start in range(0, members, group):
            values = [value_ref[(start + i, *at)] for i in range(group)]
            if start == 0:
                grads = [jnp.zeros((8, 128), F32) for _ in range(group)]
            else:
                grads = [grad_ref[(start + i, *at)] for i in range(group)]
            for i in range(group):
                for k in range(i):
                    gap = values[i] - values[k]
                    square = gap * gap + 0.25
                    inverse = lax.rsqrt(square)
                    pair = pair + inverse
                    slope = gap * inverse
                    grads[i] = grads[i] + slope
                    grads[k] = grads[k] - slope
            for m in range(start + group, members):
                other = value_ref[(m, *at)]
                if start == 0:
                    other_grad = jnp.zeros((8, 128), F32)
                else:
                    other_grad = grad_ref[(m, *at)]
                for i in range(group):
                    gap = other - values[i]
                    square = gap * gap + 0.25
                    inverse = lax.rsqrt(square)
                    pair = pair + inverse
                    slope = gap * inverse
                    other_grad = other_grad + slope
                    grads[i] = grads[i] - slope
                grad_ref[(m, *at)] = other_grad
            for i in range(group):
                miss = values[i] - truth
                square = miss * miss + 0.25
                inverse = lax.rsqrt(square)
                own = own + square * inverse
                moment = moment + values[i] * grads[i]
                answer = (miss * inverse) * (1.0 / members) + grads[i] * pair_scale
                grad_ref[(start + i, *at)] = answer * lat_weight
        pair = moment + 0.25 * pair
        return total + (own * (1.0 / members) + pair * pair_scale)

    tiles = (count // 8) * (channels // 128)
    total = lax.fori_loop(0, tiles, tile, jnp.zeros((8, 128), F32))
    loss_ref[...] = total * lat_weight
    slope_ref[...] = grad_ref[...].astype(BF16)


def call(kernel, out_shape, *operands, smem=(), smem_out=(), away=(), loose=False, scratch=(), held=()):
    spaces = [pltpu.VMEM for _ in operands]
    for i in smem:
        spaces[i] = pltpu.SMEM
    for i in away:
        spaces[i] = pl.ANY
    operands = [
        pltpu.with_memory_space_constraint(x, pltpu.VMEM)
        if space == pltpu.VMEM and not loose
        else x
        for x, space in zip(operands, spaces)
    ]
    shapes = [
        shape if loose else (pltpu.VMEM if i in held else pltpu.HBM)(shape.shape, shape.dtype)
        for i, shape in enumerate(out_shape)
    ]
    out_spaces = [pltpu.SMEM if i in smem_out else pltpu.VMEM for i in range(len(shapes))]
    return pl.pallas_call(
        kernel,
        out_shape=shapes,
        in_specs=[pl.BlockSpec(memory_space=space) for space in spaces],
        out_specs=[pl.BlockSpec(memory_space=space) for space in out_spaces],
        scratch_shapes=scratch,
        compiler_params=pltpu.CompilerParams(vmem_limit_bytes=None if loose else VMEM_LIMIT),
    )(*operands)


def reduce_weight_grad(mine, theirs, loss):
    lat_count, ens_count = lax.axis_size("lat"), lax.axis_size("ens")
    lon_index = lax.axis_index("lon")
    rows, lanes = mine.shape
    piece = rows // ens_count
    swap = [(0, 1), (1, 0)]
    arrived = lax.ppermute(theirs, "lon", swap)
    (summed,) = call(
        merge_kernel,
        (jax.ShapeDtypeStruct((ens_count, piece + 8, lanes), BF16),),
        mine,
        arrived,
        loss,
        loose=True,
    )
    summed = lax.all_to_all(summed, "ens", 0, 0, tiled=True)

    def marked(total):
        share = total[piece : piece + 1] + total[piece + 1 : piece + 2]
        blank = jnp.zeros((6, lanes), BF16)
        return jnp.concatenate([total[:piece].astype(BF16), *split(share), blank], 0)

    total = jnp.sum(summed.astype(F32), 0)
    sent = marked(total)
    arrived = [
        lax.ppermute(sent, "lat", [(i, (i + step) % lat_count) for i in range(lat_count)])
        for step in range(1, lat_count)
    ]
    for block in arrived:
        total = total + block.astype(F32)
    spread_out = jnp.broadcast_to(marked(total)[None], summed.shape)
    gathered = lax.all_to_all(spread_out, "ens", 0, 0, tiled=True)
    other = lax.ppermute(gathered, "lon", swap)
    whole, loss = call(
        whole_kernel,
        (
            jax.ShapeDtypeStruct((rows, 2 * lanes), F32),
            jax.ShapeDtypeStruct((1, 1), F32),
        ),
        gathered,
        other,
        lon_index[None],
        smem=(2,),
        smem_out=(1,),
        loose=True,
    )
    return whole, loss[0, 0]


def step(inputs, weight, spread, target):
    row_count, width, channels = inputs.shape[1:]
    reach = HMAX
    members = lax.axis_size("ens")
    lat_total = row_count * lax.axis_size("lat")
    lon_total = width * lax.axis_size("lon")
    lat_index, lon_index, ens_index = (lax.axis_index(a) for a in ("lat", "lon", "ens"))
    field = inputs[0]
    wave_cols, basis = circle_waves(lon_index, width, lon_total)
    rows_around = lat_index * row_count - 1 + jnp.arange(row_count + 2)
    polar = (rows_around < PCAP) | (rows_around >= lat_total - PCAP)
    polar_scale = polar.astype(F32)

    own = extend_lon(field, basis, spread, reach)
    low, high = lat_neighbours(own)
    own_band = band_blocks(spread, ~polar[1:3], reach)
    own_polar = polar_scale[1:3]
    cells = -(-(row_count * width // members) // 16) * 16
    (begun,) = call(
        own_rows_kernel,
        (jax.ShapeDtypeStruct((row_count, width, channels), F32),),
        own,
        weight,
        own_band,
        wave_cols,
        own_polar,
        smem=(4,),
        held=(0,),
    )
    response, sent = call(
        outer_rows_kernel,
        (
            jax.ShapeDtypeStruct((row_count, width, channels), BF16),
            jax.ShapeDtypeStruct((members * cells, channels), BF16),
        ),
        low,
        high,
        begun,
        weight,
        own_band,
        wave_cols,
        own_polar,
        smem=(6,),
    )
    everyone = lax.all_to_all(
        sent.reshape(members, cells, channels), "ens", 0, 0, tiled=True
    )
    held = row_count * width // cells
    first_cell = jnp.minimum(ens_index, held - 1) * cells
    truth = lax.dynamic_slice_in_dim(target.reshape(-1, channels), first_cell, cells, 0)
    cell_row = lat_index * row_count + first_cell // width
    row_weight = jnp.sin(math.pi * (cell_row.astype(F32) + 0.5) / lat_total)
    row_weight = jnp.where(ens_index < held, row_weight, 0.0)
    slopes, loss_tile = call(
        crps_kernel,
        (
            jax.ShapeDtypeStruct((members, cells, channels), BF16),
            jax.ShapeDtypeStruct((8, 128), F32),
        ),
        everyone,
        truth,
        row_weight[None],
        smem=(2,),
        held=(0, 1),
        scratch=[
            pltpu.VMEM((members, cells, channels), F32),
            pltpu.VMEM((members, cells, channels), F32),
        ],
    )
    slopes = lax.all_to_all(slopes, "ens", 0, 0, tiled=True)
    slopes = slopes.reshape(-1, channels)
    loss_share = jnp.sum(loss_tile, 0, keepdims=True) / (lat_total * lon_total * channels)

    slope_rows = slopes[: row_count * width].reshape(row_count, width, channels)
    slope_sums, slope_other = circle_parcel(slope_rows, basis, reach)
    scale = math.sqrt(weight.shape[0] * channels) / (lat_total * lon_total)
    half = jax.ShapeDtypeStruct((weight.shape[0] * channels, channels // 2), BF16)
    mine, theirs, slope_own = call(
        functools.partial(weight_grad_kernel, scale=scale),
        (half, half, jax.ShapeDtypeStruct((row_count, width + 3 * reach, channels), BF16)),
        slopes,
        slope_sums,
        slope_other,
        low,
        own,
        high,
        own_band,
        wave_cols,
        own_polar,
        lon_index[None],
        spread.astype(F32),
        smem=(8, 9, 10),
        away=(0, 3, 4, 5),
        loose=True,
        scratch=[
            pltpu.VMEM((row_count, width, 3 * channels), BF16),
            pltpu.VMEM((row_count + 2, width, channels), BF16),
            pltpu.SemaphoreType.DMA((6,)),
        ],
    )
    slope_low, slope_high = lat_neighbours(slope_own)
    grad_weight, loss = reduce_weight_grad(mine, theirs, loss_share)
    around = jnp.stack([low[0, -1, 0], high[0, -1, 0]]).astype(spread.dtype)
    all_spread = jnp.concatenate([around[:1], spread, around[1:]])
    (grad_input,) = call(
        input_grad_kernel,
        (jax.ShapeDtypeStruct((row_count, width, channels), BF16),),
        slope_low,
        slope_own,
        slope_high,
        weight,
        band_blocks(all_spread, ~polar, reach),
        wave_cols,
        polar_scale,
        smem=(6,),
        loose=True,
        scratch=[pltpu.VMEM((row_count, width, channels), F32)],
    )
    return (response[None], grad_input[None], grad_weight.reshape(weight.shape), loss)


def solution(mesh):
    in_specs = (P("ens", "lat", "lon", None), P(), P("lat"), P("lat", "lon", None))
    out_specs = (P("ens", "lat", "lon", None), P("ens", "lat", "lon", None), P(), P())
    return jax.shard_map(step, mesh=mesh, in_specs=in_specs, out_specs=out_specs, check_vma=False)
```

time: 742 us -> 186 us (0.25)
  the two profiles are of different devices: /device:TPU:2 before, /device:TPU:1 now
where the time goes in v1:
time: 186 us; the launch traced here: 185 us
  waiting for transfers between devices  59.3 us (32%)
  starting transfers between devices  44.7 us (24%)
  Pallas kernels  35 us (19%)
  blocking collectives  25.4 us (14%)
  local copies, waits for them, and re-layouts  8.84 us (5%)
  other arithmetic  8.62 us (5%)
    pallas_call x7, Pallas kernels, call(): pl.pallas_call(kernel, out_shape=shapes, in_specs=[pl.BlockSpec(memory_sp...  35 us
    all_to_all x1, blocking collectives, step(): slopes = lax.all_to_all(slopes, 'ens', 0, 0, tiled=True)  25.4 us
    all_to_all x1, waiting for transfers between devices, step(): lax.all_to_all(sent.reshape(members, cells, channels), 'ens', 0, 0, tiled...  20.9 us
    all_to_all x1, waiting for transfers between devices, reduce_weight_grad(): summed = lax.all_to_all(summed, 'ens', 0, 0, tiled=True)  18.8 us
    all_to_all x1, starting transfers between devices, step(): lax.all_to_all(sent.reshape(members, cells, channels), 'ens', 0, 0, tiled...  11.2 us
    ppermute x2, starting transfers between devices, circle_parcel(): return (sums, lax.ppermute(parcel, 'lon', [(0, 1), (1, 0)]))  7.57 us
    all_to_all x1, waiting for transfers between devices, reduce_weight_grad(): gathered = lax.all_to_all(spread_out, 'ens', 0, 0, tiled=True)  7.02 us
    all_to_all x1, starting transfers between devices, reduce_weight_grad(): gathered = lax.all_to_all(spread_out, 'ens', 0, 0, tiled=True)  5.93 us
  transfers between devices with their start and end apart: 14, of which 9 were waited for; matrix products, arithmetic and copies ran while one was open for 6% of the time, Pallas kernels for 6%

profile of v1, /device:TPU:1, one launch (start us, length us, event | category | flops | bytes accessed | tf_op | source)
XLA Modules:
  0.0 184.9 jit_solution(13202676083067371921)
XLA Ops:
  0.7 1.5 convolution_bitcast_fusion.1
  2.2 0.7 fusion.19
  3.0 0.2 concatenate.29
  3.1 3.3 %collective-permute-start = (bf16[2,48,256]{2,1,0:T(8,128)(2,1)S(1)}, bf16[2,48,256]{2,1,0:T(8,128)(2,1)S(1)}, u32[]{:S(2)}, u32[]{:S(2)}) collective-permute-start(bf16[2,48,256]{2,1,0:T(8,128)(2,1)S(1)} %concatenate.29), channel_id=1, source_target_pairs={{0,32},{32,0},{1,33},{33,1},{2,34},{34,2},{3,35},{35,3},{4,36},{36... | collective-permute-start | bytes 147464 | tf_op jit(solution)/shard_map/ppermute | solution.py:62
  6.4 1.2 fusion.22
  7.7 0.7 fusion.11
  8.4 0.1 slice_not_fusion
  8.5 0.8 dynamic-slice_bitcast_fusion.wave_ref
  9.2 0.1 broadcast_multiply_fusion.1
  9.3 0.1 slice.108.flag_ref
  9.4 0.1 broadcast_in_dim.44
  9.5 0.4 concatenate.30.own_ref
  9.9 0.1 fusion.17
  10.0 1.6 collective-permute-start.1
  11.5 1.3 collective-permute-start.2
  12.8 0.4 select_convert_fusion.1.band_ref
  13.3 3.6 %shard_map.93.begun_ref = f32[2,720,256]{2,1,0:T(8,128)S(1)} custom-call(bf16[2,768,256]{2,1,0:T(8,128)(2,1)S(1)} %concatenate.30.own_ref, bf16[9,256,256]{2,1,0:T(8,128)(2,1)S(1)} %copy-done.3, bf16[2,3,224,256]{3,2,1,0:T(8,128)(2,1)S(1)} %select_convert_fusion.1.band_ref, f32[720,2]{1,0:T(8,128)S(1)} %copy-done.4, f32[2]{0:T(128)S(1)} %slice.108.flag_ref), custom_call_target="tpu_custom_call" | custom-call | tf_op jit(solution)/shard_map/pallas_call | solution.py:377
  16.9 3.1 %collective-permute-done.1.low_ref = bf16[1,768,256]{2,1,0:T(8,128)(2,1)S(1)} collective-permute-done((bf16[1,768,256]{2,1,0:T(8,128)(2,1)S(1)}, bf16[1,768,256]{2,1,0:T(8,128)(2,1)S(1)}, u32[]{:S(2)}, u32[]{:S(2)}) %collective-permute-start.1) | collective-permute-done | bytes 393248 | tf_op jit(solution)/shard_map/ppermute | solution.py:79
  20.0 3.9 %collective-permute-done.2.high_ref = bf16[1,768,256]{2,1,0:T(8,128)(2,1)S(1)} collective-permute-done((bf16[1,768,256]{2,1,0:T(8,128)(2,1)S(1)}, bf16[1,768,256]{2,1,0:T(8,128)(2,1)S(1)}, u32[]{:S(2)}, u32[]{:S(2)}) %collective-permute-start.2) | collective-permute-done | bytes 393248 | tf_op jit(solution)/shard_map/ppermute | solution.py:80
  23.8 3.9 %shard_map.94 = (bf16[2,720,256]{2,1,0:T(8,128)(2,1)}, bf16[1536,256]{1,0:T(8,128)(2,1)}) custom-call(bf16[1,768,256]{2,1,0:T(8,128)(2,1)S(1)} %collective-permute-done.1.low_ref, bf16[1,768,256]{2,1,0:T(8,128)(2,1)S(1)} %collective-permute-done.2.high_ref, f32[2,720,256]{2,1,0:T(8,128)S(1)} %shard_map.93.begun_ref, bf16[9,256,256]{2,1,0:T(8,128)(2,1)S(1)} %copy-done.3, ...), custom_call_target="tpu_custom_call" | custom-call | tf_op jit(solution)/shard_map/pallas_call | solution.py:377
  27.7 11.2 %all-to-all-start = ((bf16[32,48,256]{2,1,0:T(8,128)(2,1)}), bf16[32,48,256]{2,1,0:T(8,128)(2,1)S(1)}, u32[]{:S(2)}, u32[]{:S(2)}) async-start(bf16[32,48,256]{2,1,0:T(8,128)(2,1)} %bitcast.36), calls=%async_computation | async-start | bytes 1572864 | tf_op jit(solution)/shard_map/all_to_all | solution.py:480
  39.1 20.9 %all-to-all-done.z_ref = bf16[32,48,256]{2,1,0:T(8,128)(2,1)S(1)} async-done(((bf16[32,48,256]{2,1,0:T(8,128)(2,1)}), bf16[32,48,256]{2,1,0:T(8,128)(2,1)S(1)}, u32[]{:S(2)}, u32[]{:S(2)}) %all-to-all-start) | async-done | bytes 786464 | tf_op jit(solution)/shard_map/all_to_all | solution.py:480
  60.0 7.3 %shard_map.95 = (bf16[32,48,256]{2,1,0:T(8,128)(2,1)S(1)}, f32[8,128]{1,0:T(8,128)S(1)}) custom-call(bf16[32,48,256]{2,1,0:T(8,128)(2,1)S(1)} %all-to-all-done.z_ref, bf16[48,256]{1,0:T(8,128)(2,1)S(1)} %constant_dynamic-slice_fusion.truth_ref, f32[1]{0:T(128)} %bitcast.8.weight_ref), custom_call_target="tpu_custom_call" | custom-call | tf_op jit(solution)/shard_map/pallas_call | solution.py:377
  67.3 25.4 %all_to_all.20 = bf16[32,48,256]{2,1,0:T(8,128)(2,1)S(1)} all-to-all(bf16[32,48,256]{2,1,0:T(8,128)(2,1)S(1)} %get-tuple-element.15), channel_id=1, replica_groups=mesh['lat'=4,'lon'=2,'ens'=32] {'ens'}, dimensions={0} | all-to-all | bytes 1572864 | tf_op jit(solution)/shard_map/all_to_all | solution.py:505
  92.7 0.2 convolution_bitcast_fusion
  93.0 0.6 fusion.6
  93.6 0.2 concatenate.32
  93.7 4.3 %collective-permute-start.3 = (bf16[2,48,256]{2,1,0:T(8,128)(2,1)S(1)}, bf16[2,48,256]{2,1,0:T(8,128)(2,1)S(1)}, u32[]{:S(2)}, u32[]{:S(2)}) collective-permute-start(bf16[2,48,256]{2,1,0:T(8,128)(2,1)S(1)} %concatenate.32), channel_id=1, source_target_pairs={{0,32},{32,0},{1,33},{33,1},{2,34},{34,2},{3,35},{35,3},{4,36},{36... | collective-permute-start | bytes 147464 | tf_op jit(solution)/shard_map/ppermute | solution.py:62
  98.0 0.9 collective-permute-done.3.other_ref
  98.9 0.6 copy-done.15
  99.5 8.2 %shard_map.96 = (bf16[2304,128]{1,0:T(8,128)(2,1)}, bf16[2304,128]{1,0:T(8,128)(2,1)}, bf16[2,768,256]{2,1,0:T(8,128)(2,1)}) custom-call(bf16[1536,256]{1,0:T(8,128)(2,1)} %bitcast.31, f32[2,3,256]{2,1,0:T(4,128)} %get-tuple-element.40.sums_ref, bf16[2,48,256]{2,1,0:T(8,128)(2,1)} %copy-done.15, bf16[1,768,256]{2,1,0:T(8,128)(2,1)} %copy-done.5, ...), custom_call_target="tpu_custom_call" | custom-call | tf_op jit(solution)/shard_map/pallas_call | solution.py:377
  107.8 0.5 collective-permute-start.6
  108.2 0.5 multiply_bitcast_fusion.loss_ref
  108.8 1.3 collective-permute-done.6.theirs_ref
  110.1 0.8 copy-done.13
  110.9 2.2 %shard_map.98 = bf16[32,80,128]{2,1,0:T(8,128)(2,1)} custom-call(bf16[2304,128]{1,0:T(8,128)(2,1)} %get-tuple-element.17.mine_ref, bf16[2304,128]{1,0:T(8,128)(2,1)} %copy-done.13, f32[1,128]{1,0:T(1,128)} %multiply_bitcast_fusion.loss_ref), custom_call_target="tpu_custom_call" | custom-call | tf_op jit(solution)/shard_map/pallas_call | solution.py:377
  113.1 4.8 %all-to-all-start.2 = ((bf16[32,80,128]{2,1,0:T(8,128)(2,1)}), bf16[32,80,128]{2,1,0:T(8,128)(2,1)S(1)}, u32[]{:S(2)}, u32[]{:S(2)}) async-start(bf16[32,80,128]{2,1,0:T(8,128)(2,1)} %shard_map.98), calls=%async_computation.2 | async-start | bytes 1310720 | tf_op jit(solution)/shard_map/all_to_all | solution.py:402
  117.9 0.1 pad.7.clone
  118.0 18.8 %all-to-all-done.2 = bf16[32,80,128]{2,1,0:T(8,128)(2,1)S(1)} async-done(((bf16[32,80,128]{2,1,0:T(8,128)(2,1)}), bf16[32,80,128]{2,1,0:T(8,128)(2,1)S(1)}, u32[]{:S(2)}, u32[]{:S(2)}) %all-to-all-start.2) | async-done | bytes 655392 | tf_op jit(solution)/shard_map/all_to_all | solution.py:402
  136.7 0.1 convert_reduce_fusion
  136.8 0.1 maximum_maximum_fusion
  136.9 0.5 collective-permute-start.9
  137.5 2.4 %collective-permute-start.8 = (bf16[80,128]{1,0:T(8,128)(2,1)S(1)}, bf16[80,128]{1,0:T(8,128)(2,1)S(1)}, u32[]{:S(2)}, u32[]{:S(2)}) collective-permute-start(bf16[80,128]{1,0:T(8,128)(2,1)S(1)} %maximum_maximum_fusion), channel_id=1, source_target_pairs={{0,128},{64,192},{128,0},{192,64},{1,129},{65,193},{129,1},{193,65... | collective-permute-start | bytes 61448 | tf_op jit(solution)/shard_map/ppermute | solution.py:412
  139.9 0.3 collective-permute-start.7
  140.2 1.4 collective-permute-done.8
  141.6 2.2 %collective-permute-done.7 = bf16[80,128]{1,0:T(8,128)(2,1)S(1)} collective-permute-done((bf16[80,128]{1,0:T(8,128)(2,1)S(1)}, bf16[80,128]{1,0:T(8,128)(2,1)S(1)}, u32[]{:S(2)}, u32[]{:S(2)}) %collective-permute-start.7) | collective-permute-done | bytes 20512 | tf_op jit(solution)/shard_map/ppermute | solution.py:412
  143.8 0.1 maximum_maximum_fusion.1
  143.9 0.9 broadcast_in_dim.81
  144.8 5.9 %all-to-all-start.3 = ((bf16[32,80,128]{2,1,0:T(8,128)(2,1)}), bf16[32,80,128]{2,1,0:T(8,128)(2,1)S(1)}, u32[]{:S(2)}, u32[]{:S(2)}) async-start(bf16[32,80,128]{2,1,0:T(8,128)(2,1)} %broadcast_in_dim.81), calls=%async_computation.3 | async-start | bytes 1310720 | tf_op jit(solution)/shard_map/all_to_all | solution.py:418
  150.7 1.2 slice.145
  151.9 1.2 slice.144
  153.1 1.4 maximum_convert_fusion
  154.5 0.6 fusion.21
  155.1 1.4 fusion.12
  156.4 0.1 broadcast_multiply_fusion
  156.5 0.1 fusion.16
  156.6 2.0 %collective-permute-start.4 = (bf16[1,768,256]{2,1,0:T(8,128)(2,1)S(1)}, bf16[1,768,256]{2,1,0:T(8,128)(2,1)}, u32[]{:S(2)}, u32[]{:S(2)}) collective-permute-start(bf16[1,768,256]{2,1,0:T(8,128)(2,1)S(1)} %get-tuple-element.23), channel_id=1, source_target_pairs={{0,64},{64,128},{128,192},{1,65},{65,129},{129,193},{2,66},{66,130... | collective-permute-start | bytes 1179656 | tf_op jit(solution)/shard_map/ppermute | solution.py:79
  158.6 1.3 collective-permute-start.5
  159.9 7.0 %all-to-all-done.3.own_ref = bf16[32,80,128]{2,1,0:T(8,128)(2,1)S(1)} async-done(((bf16[32,80,128]{2,1,0:T(8,128)(2,1)}), bf16[32,80,128]{2,1,0:T(8,128)(2,1)S(1)}, u32[]{:S(2)}, u32[]{:S(2)}) %all-to-all-start.3) | async-done | bytes 655392 | tf_op jit(solution)/shard_map/all_to_all | solution.py:418
  166.9 5.3 %collective-permute-start.10 = (bf16[32,80,128]{2,1,0:T(8,128)(2,1)S(1)}, bf16[32,80,128]{2,1,0:T(8,128)(2,1)S(1)}, u32[]{:S(2)}, u32[]{:S(2)}) collective-permute-start(bf16[32,80,128]{2,1,0:T(8,128)(2,1)S(1)} %all-to-all-done.3.own_ref), channel_id=1, source_target_pairs={{0,32},{32,0},{1,33},{33,1},{2,34},{34,2},{3,35},{35,3},{4,36},{36... | collective-permute-start | bytes 1966088 | tf_op jit(solution)/shard_map/ppermute | solution.py:419
  172.2 1.8 select_convert_fusion.band_ref
  174.1 7.0 %shard_map.97 = bf16[2,720,256]{2,1,0:T(8,128)(2,1)} custom-call(bf16[1,768,256]{2,1,0:T(8,128)(2,1)} %collective-permute-done.4.low_ref, bf16[2,768,256]{2,1,0:T(8,128)(2,1)} %get-tuple-element.16.own_ref, bf16[1,768,256]{2,1,0:T(8,128)(2,1)} %collective-permute-done.5.high_ref, bf16[9,256,256]{2,1,0:T(8,128)(2,1)} %weight_ref.5, ...), custom_call_target="tpu_custom_call" | custom-call | tf_op jit(solution)/shard_map/pallas_call | solution.py:377
  181.0 0.8 copy-done.12
  181.9 2.9 %shard_map.99 = (f32[2304,256]{1,0:T(8,128)}, f32[1,1]{1,0:T(1,128)}) custom-call(bf16[32,80,128]{2,1,0:T(8,128)(2,1)} %copy-done.11, bf16[32,80,128]{2,1,0:T(8,128)(2,1)} %copy-done.12, s32[1]{0:T(128)} %bitcast.12.lon_ref), custom_call_target="tpu_custom_call" | custom-call | tf_op jit(solution)/shard_map/pallas_call | solution.py:377
  (64 shorter events, 0.4 us)
Async XLA Ops:
  0.6 38.4 %copy-start = (bf16[2,720,256]{2,1,0:T(8,128)(2,1)S(1)}, bf16[2,720,256]{2,1,0:T(8,128)(2,1)}, u32[]{:S(2)}) copy-start(bf16[2,720,256]{2,1,0:T(8,128)(2,1)} %param.9) | copy-start | bytes 2211844
  0.6 7.8 %copy-start.14 = (f32[2,720,2]{2,1,0:T(8,128)S(1)}, f32[2,720,2]{2,1,0:T(8,128)}, u32[]{:S(2)}) copy-start(f32[2,720,2]{2,1,0:T(8,128)} %constant.87.clone) | copy-start | bytes 34564
  0.7 8.8 %copy-start.10 = (bf16[1,2,720,256]{3,2,1,0:T(8,128)(2,1)S(1)}, bf16[1,2,720,256]{3,2,1,0:T(8,128)(2,1)}, u32[]{:S(2)}) copy-start(bf16[1,2,720,256]{3,2,1,0:T(8,128)(2,1)} %param.6) | copy-start | bytes 2211844
  3.1 6.2 %collective-permute-start = (bf16[2,48,256]{2,1,0:T(8,128)(2,1)S(1)}, bf16[2,48,256]{2,1,0:T(8,128)(2,1)S(1)}, u32[]{:S(2)}, u32[]{:S(2)}) collective-permute-start(bf16[2,48,256]{2,1,0:T(8,128)(2,1)S(1)} %concatenate.29), channel_id=1, source_target_pairs={{0,32},{32,0},{1,33},{33,1},{2,34},{34,2},{3,35},{35,3},{4,36},{36... | collective-permute-start | bytes 147464 | tf_op jit(solution)/shard_map/ppermute | solution.py:62
  9.3 0.7 copy-start.18
  9.4 14.5 %copy-start.7 = (f32[2]{0:T(128)}, f32[2]{0:T(128)S(1)}, u32[]{:S(2)}) copy-start(f32[2]{0:T(128)S(1)} %slice.108.flag_ref) | copy-start | bytes 28
  9.9 7.0 %copy-start.1 = (bf16[2,768,256]{2,1,0:T(8,128)(2,1)}, bf16[2,768,256]{2,1,0:T(8,128)(2,1)S(1)}, u32[]{:S(2)}) copy-start(bf16[2,768,256]{2,1,0:T(8,128)(2,1)S(1)} %concatenate.30.own_ref) | copy-start | bytes 2359300
  9.9 3.4 %copy-start.3 = (bf16[9,256,256]{2,1,0:T(8,128)(2,1)S(1)}, bf16[9,256,256]{2,1,0:T(8,128)(2,1)}, u32[]{:S(2)}) copy-start(bf16[9,256,256]{2,1,0:T(8,128)(2,1)} %weight_ref.5) | copy-start | bytes 3538948
  9.9 3.4 %copy-start.4 = (f32[720,2]{1,0:T(8,128)S(1)}, f32[720,2]{1,0:T(8,128)}, u32[]{:S(2)}) copy-start(f32[720,2]{1,0:T(8,128)} %dynamic-slice_bitcast_fusion.wave_ref) | copy-start | bytes 17284
  10.0 10.0 %collective-permute-start.1 = (bf16[1,768,256]{2,1,0:T(8,128)(2,1)S(1)}, bf16[1,768,256]{2,1,0:T(8,128)(2,1)S(1)}, u32[]{:S(2)}, u32[]{:S(2)}) collective-permute-start(bf16[1,768,256]{2,1,0:T(8,128)(2,1)S(1)} %get-tuple-element.25), channel_id=1, source_target_pairs={{0,64},{64,128},{128,192},{1,65},{65,129},{129,193},{2,66},{66,130... | collective-permute-start | bytes 1179656 | tf_op jit(solution)/shard_map/ppermute | solution.py:79
  11.5 12.3 %collective-permute-start.2 = (bf16[1,768,256]{2,1,0:T(8,128)(2,1)S(1)}, bf16[1,768,256]{2,1,0:T(8,128)(2,1)S(1)}, u32[]{:S(2)}, u32[]{:S(2)}) collective-permute-start(bf16[1,768,256]{2,1,0:T(8,128)(2,1)S(1)} %get-tuple-element.24), channel_id=1, source_target_pairs={{64,0},{128,64},{192,128},{65,1},{129,65},{193,129},{66,2},{130,66... | collective-permute-start | bytes 1179656 | tf_op jit(solution)/shard_map/ppermute | solution.py:80
  13.3 10.5 %copy-start.2 = (bf16[2,3,224,256]{3,2,1,0:T(8,128)(2,1)}, bf16[2,3,224,256]{3,2,1,0:T(8,128)(2,1)S(1)}, u32[]{:S(2)}) copy-start(bf16[2,3,224,256]{3,2,1,0:T(8,128)(2,1)S(1)} %select_convert_fusion.1.band_ref) | copy-start | bytes 2064388
  20.0 7.8 %copy-start.5 = (bf16[1,768,256]{2,1,0:T(8,128)(2,1)}, bf16[1,768,256]{2,1,0:T(8,128)(2,1)S(1)}, u32[]{:S(2)}) copy-start(bf16[1,768,256]{2,1,0:T(8,128)(2,1)S(1)} %collective-permute-done.1.low_ref) | copy-start | bytes 1179652
  23.8 3.9 %copy-start.6 = (bf16[1,768,256]{2,1,0:T(8,128)(2,1)}, bf16[1,768,256]{2,1,0:T(8,128)(2,1)S(1)}, u32[]{:S(2)}) copy-start(bf16[1,768,256]{2,1,0:T(8,128)(2,1)S(1)} %collective-permute-done.2.high_ref) | copy-start | bytes 1179652
  27.7 32.2 %all-to-all-start = ((bf16[32,48,256]{2,1,0:T(8,128)(2,1)}), bf16[32,48,256]{2,1,0:T(8,128)(2,1)S(1)}, u32[]{:S(2)}, u32[]{:S(2)}) async-start(bf16[32,48,256]{2,1,0:T(8,128)(2,1)} %bitcast.36), calls=%async_computation | async-start | bytes 1572864 | tf_op jit(solution)/shard_map/all_to_all | solution.py:480
  67.3 25.5 %copy-start.16 = (bf16[2,5,720]{2,1,0:T(8,128)(2,1)S(1)}, bf16[2,5,720]{2,1,0:T(8,128)(2,1)}, u32[]{:S(2)}) copy-start(bf16[2,5,720]{2,1,0:T(8,128)(2,1)} %constant.88.clone) | copy-start | bytes 43204
  92.7 6.2 %copy-start.8 = (bf16[32,48,256]{2,1,0:T(8,128)(2,1)}, bf16[32,48,256]{2,1,0:T(8,128)(2,1)S(1)}, u32[]{:S(2)}) copy-start(bf16[32,48,256]{2,1,0:T(8,128)(2,1)S(1)} %all_to_all.20) | copy-start | bytes 2359300
  93.7 5.2 %collective-permute-start.3 = (bf16[2,48,256]{2,1,0:T(8,128)(2,1)S(1)}, bf16[2,48,256]{2,1,0:T(8,128)(2,1)S(1)}, u32[]{:S(2)}, u32[]{:S(2)}) collective-permute-start(bf16[2,48,256]{2,1,0:T(8,128)(2,1)S(1)} %concatenate.32), channel_id=1, source_target_pairs={{0,32},{32,0},{1,33},{33,1},{2,34},{34,2},{3,35},{35,3},{4,36},{36... | collective-permute-start | bytes 147464 | tf_op jit(solution)/shard_map/ppermute | solution.py:62
  98.9 0.6 copy-start.15
  107.8 2.3 %collective-permute-start.6 = (bf16[2304,128]{1,0:T(8,128)(2,1)}, bf16[2304,128]{1,0:T(8,128)(2,1)S(1)}, u32[]{:S(2)}, u32[]{:S(2)}) collective-permute-start(bf16[2304,128]{1,0:T(8,128)(2,1)} %get-tuple-element.18), channel_id=1, source_target_pairs={{0,32},{32,0},{1,33},{33,1},{2,34},{34,2},{3,35},{35,3},{4,36},{36... | collective-permute-start | bytes 1769480 | tf_op jit(solution)/shard_map/ppermute | solution.py:393
  110.1 0.8 copy-start.13
  113.1 23.6 %all-to-all-start.2 = ((bf16[32,80,128]{2,1,0:T(8,128)(2,1)}), bf16[32,80,128]{2,1,0:T(8,128)(2,1)S(1)}, u32[]{:S(2)}, u32[]{:S(2)}) async-start(bf16[32,80,128]{2,1,0:T(8,128)(2,1)} %shard_map.98), calls=%async_computation.2 | async-start | bytes 1310720 | tf_op jit(solution)/shard_map/all_to_all | solution.py:402
  118.0 37.1 %copy-start.17 = (s32[2]{0:T(128)S(1)}, s32[2]{0:T(128)}, u32[]{:S(2)}) copy-start(s32[2]{0:T(128)} %param.8) | copy-start | bytes 28
  118.0 38.6 %copy-start.9 = (bf16[2,768,256]{2,1,0:T(8,128)(2,1)S(1)}, bf16[2,768,256]{2,1,0:T(8,128)(2,1)}, u32[]{:S(2)}) copy-start(bf16[2,768,256]{2,1,0:T(8,128)(2,1)} %get-tuple-element.16.own_ref) | copy-start | bytes 2359300
  136.9 3.3 %collective-permute-start.9 = (bf16[80,128]{1,0:T(8,128)(2,1)S(1)}, bf16[80,128]{1,0:T(8,128)(2,1)S(1)}, u32[]{:S(2)}, u32[]{:S(2)}) collective-permute-start(bf16[80,128]{1,0:T(8,128)(2,1)S(1)} %maximum_maximum_fusion), channel_id=1, source_target_pairs={{0,192},{64,0},{128,64},{192,128},{1,193},{65,1},{129,65},{193,129... | collective-permute-start | bytes 61448 | tf_op jit(solution)/shard_map/ppermute | solution.py:412
  137.5 4.1 %collective-permute-start.8 = (bf16[80,128]{1,0:T(8,128)(2,1)S(1)}, bf16[80,128]{1,0:T(8,128)(2,1)S(1)}, u32[]{:S(2)}, u32[]{:S(2)}) collective-permute-start(bf16[80,128]{1,0:T(8,128)(2,1)S(1)} %maximum_maximum_fusion), channel_id=1, source_target_pairs={{0,128},{64,192},{128,0},{192,64},{1,129},{65,193},{129,1},{193,65... | collective-permute-start | bytes 61448 | tf_op jit(solution)/shard_map/ppermute | solution.py:412
  139.9 3.8 %collective-permute-start.7 = (bf16[80,128]{1,0:T(8,128)(2,1)S(1)}, bf16[80,128]{1,0:T(8,128)(2,1)S(1)}, u32[]{:S(2)}, u32[]{:S(2)}) collective-permute-start(bf16[80,128]{1,0:T(8,128)(2,1)S(1)} %maximum_maximum_fusion), channel_id=1, source_target_pairs={{0,64},{64,128},{128,192},{192,0},{1,65},{65,129},{129,193},{193,1... | collective-permute-start | bytes 61448 | tf_op jit(solution)/shard_map/ppermute | solution.py:412
  144.8 22.1 %all-to-all-start.3 = ((bf16[32,80,128]{2,1,0:T(8,128)(2,1)}), bf16[32,80,128]{2,1,0:T(8,128)(2,1)S(1)}, u32[]{:S(2)}, u32[]{:S(2)}) async-start(bf16[32,80,128]{2,1,0:T(8,128)(2,1)} %broadcast_in_dim.81), calls=%async_computation.3 | async-start | bytes 1310720 | tf_op jit(solution)/shard_map/all_to_all | solution.py:418
  156.6 17.5 %collective-permute-start.4 = (bf16[1,768,256]{2,1,0:T(8,128)(2,1)S(1)}, bf16[1,768,256]{2,1,0:T(8,128)(2,1)}, u32[]{:S(2)}, u32[]{:S(2)}) collective-permute-start(bf16[1,768,256]{2,1,0:T(8,128)(2,1)S(1)} %get-tuple-element.23), channel_id=1, source_target_pairs={{0,64},{64,128},{128,192},{1,65},{65,129},{129,193},{2,66},{66,130... | collective-permute-start | bytes 1179656 | tf_op jit(solution)/shard_map/ppermute | solution.py:79
  158.6 15.4 %collective-permute-start.5 = (bf16[1,768,256]{2,1,0:T(8,128)(2,1)S(1)}, bf16[1,768,256]{2,1,0:T(8,128)(2,1)}, u32[]{:S(2)}, u32[]{:S(2)}) collective-permute-start(bf16[1,768,256]{2,1,0:T(8,128)(2,1)S(1)} %get-tuple-element.22), channel_id=1, source_target_pairs={{64,0},{128,64},{192,128},{65,1},{129,65},{193,129},{66,2},{130,66... | collective-permute-start | bytes 1179656 | tf_op jit(solution)/shard_map/ppermute | solution.py:80
  166.9 14.1 %copy-start.11 = (bf16[32,80,128]{2,1,0:T(8,128)(2,1)}, bf16[32,80,128]{2,1,0:T(8,128)(2,1)S(1)}, u32[]{:S(2)}) copy-start(bf16[32,80,128]{2,1,0:T(8,128)(2,1)S(1)} %all-to-all-done.3.own_ref) | copy-start | bytes 1966084
  166.9 14.1 %collective-permute-start.10 = (bf16[32,80,128]{2,1,0:T(8,128)(2,1)S(1)}, bf16[32,80,128]{2,1,0:T(8,128)(2,1)S(1)}, u32[]{:S(2)}, u32[]{:S(2)}) collective-permute-start(bf16[32,80,128]{2,1,0:T(8,128)(2,1)S(1)} %all-to-all-done.3.own_ref), channel_id=1, source_target_pairs={{0,32},{32,0},{1,33},{33,1},{2,34},{34,2},{3,35},{35,3},{4,36},{36... | collective-permute-start | bytes 1966088 | tf_op jit(solution)/shard_map/ppermute | solution.py:419
  181.0 0.8 copy-start.12

commit v2 on v1

--- a/solution.py
+++ b/solution.py
@@ -35,7 +35,8 @@
     columns = both.T.astype(np.float32).reshape(-1, lon_count, 2)
     basis = basis.reshape(5, -1, lon_count).transpose(1, 0, 2)
     pick = functools.partial(lax.dynamic_index_in_dim, index=lon_index, axis=0, keepdims=False)
-    return pick(jnp.asarray(columns)), pick(jnp.asarray(basis))
+    basis = jnp.asarray(basis)
+    return pick(jnp.asarray(columns)), pick(basis), basis
 
 
 def blocks(width):
@@ -62,16 +63,42 @@
     return sums, lax.ppermute(parcel, "lon", [(0, 1), (1, 0)])
 
 
-def extend_lon(rows, basis, spread_rows, reach):
-    count, _, channels = rows.shape
-    sums, other = circle_parcel(rows, basis, reach)
-    total = sums + other[:, 2 * reach : 2 * reach + 3].astype(F32)
-    total = total + other[:, 2 * reach + 3 : 2 * reach + 6].astype(F32)
-    high, low = split(total)
-    mark = jnp.broadcast_to(spread_rows.astype(BF16)[:, None, None], (count, reach - 6, channels))
-    return jnp.concatenate(
-        [other[:, reach : 2 * reach], rows, other[:, :reach], high, low, mark], 1
-    )
+def parcel_kernel(field_ref, basis_ref, lon_ref, sums_ref, parcel_ref):
+    width, channels = field_ref.shape[1:]
+    reach = HMAX
+    basis = basis_ref[lon_ref[0]]
+    for row in range(2):
+        parts = dot(basis, field_ref[row], 1, 0)
+        sums = jnp.concatenate([parts[:2] + parts[3:5], parts[2:3]], 0)
+        high = sums.astype(BF16)
+        low = (sums - high.astype(F32)).astype(BF16)
+        sums_ref[row] = sums
+        parcel_ref[row, :reach] = field_ref[row, :reach]
+        parcel_ref[row, reach : 2 * reach] = field_ref[row, width - reach :]
+        parcel_ref[row, 2 * reach :] = jnp.concatenate(
+            [high, low, jnp.zeros((reach - 6, channels), BF16)], 0
+        )
+
+
+def fill_edges(ext_ref, sums, other_ref, spread_row):
+    reach = HMAX
+    channels = ext_ref.shape[1]
+    width = ext_ref.shape[0] - 3 * reach
+    total = sums + other_ref[2 * reach : 2 * reach + 3].astype(F32)
+    total = total + other_ref[2 * reach + 3 : 2 * reach + 6].astype(F32)
+    high = total.astype(BF16)
+    low = (total - high.astype(F32)).astype(BF16)
+    mark = jnp.full((reach - 6, channels), spread_row, F32).astype(BF16)
+    ext_ref[:reach] = other_ref[reach : 2 * reach]
+    ext_ref[reach + width : 2 * reach + width] = other_ref[:reach]
+    ext_ref[2 * reach + width :] = jnp.concatenate([high, low, mark], 0)
+
+
+def extend_kernel(field_ref, sums_ref, other_ref, spread_ref, ext_ref):
+    width = field_ref.shape[1]
+    for row in range(2):
+        fill_edges(ext_ref.at[row], sums_ref[row], other_ref.at[row], spread_ref[row])
+        ext_ref[row, HMAX : HMAX + width] = field_ref[row]
 
 
 def lat_neighbours(rows):
@@ -187,6 +214,7 @@
     ext_ref,
     back_ref,
     field_ref,
+    both_ref,
     sems,
     *,
     scale,
@@ -206,14 +234,7 @@
     for copy in copies:
         copy.start()
     for row in range(2):
-        total = sums_ref[row] + other_ref[row, 2 * reach : 2 * reach + 3].astype(F32)
-        total = total + other_ref[row, 2 * reach + 3 : 2 * reach + 6].astype(F32)
-        high = total.astype(BF16)
-        low = (total - high.astype(F32)).astype(BF16)
-        mark = jnp.full((reach - 6, channels), spread_ref[row], F32).astype(BF16)
-        ext_ref[row, :reach] = other_ref[row, reach : 2 * reach]
-        ext_ref[row, reach + width : 2 * reach + width] = other_ref[row, :reach]
-        ext_ref[row, 2 * reach + width :] = jnp.concatenate([high, low, mark], 0)
+        fill_edges(ext_ref.at[row], sums_ref[row], other_ref.at[row], spread_ref[row])
     for row in range(2):
         copies[row].wait()
         backs = spread_back_rows(ext_ref.at[row], row, band_ref, wave_ref, flag_ref[row])
@@ -232,16 +253,17 @@
                 owner, at = divmod(first + start, half)
                 for side in range(2):
                     left = shape * channels + side * lanes
-                    piece = part[start : start + channels // 2, left : left + lanes]
-                    into = pl.ds(side * half + at, channels // 2)
-
-                    @pl.when(lon_ref[0] == owner)
-                    def _():
-                        mine_ref[into] = piece
-
-                    @pl.when(lon_ref[0] != owner)
-                    def _():
-                        theirs_ref[into] = piece
+                    which = lon_ref[0] if owner == 0 else 1 - lon_ref[0]
+                    into = (which, pl.ds(side * half + at, channels // 2))
+                    both_ref[into] = part[start : start + channels // 2, left : left + lanes]
+    leave = [
+        pltpu.make_async_copy(both_ref.at[0], mine_ref, sems.at[6]),
+        pltpu.make_async_copy(both_ref.at[1], theirs_ref, sems.at[7]),
+    ]
+    for copy in leave:
+        copy.start()
+    for copy in leave:
+        copy.wait()
 
 
 def merge_kernel(mine_ref, theirs_ref, loss_ref, out_ref):
@@ -259,19 +281,16 @@
         out_ref[i, piece:] = mark
 
 
-def whole_kernel(own_ref, other_ref, lon_ref, out_ref, loss_ref):
-    count, _, lanes = own_ref.shape
+def whole_kernel(own_ref, other_ref, lon_ref, out_ref):
+    count, piece, lanes = own_ref.shape
     half = out_ref.shape[0] // 2
     side_count = count // 2
-    piece = half // side_count
     for source, owner in ((own_ref, lon_ref[0]), (other_ref, 1 - lon_ref[0])):
         base = owner * half
         for i in range(count):
             side, at = divmod(i, side_count)
             into = pl.ds(pl.multiple_of(base + at * piece, 8), piece)
-            out_ref[into, side * lanes : (side + 1) * lanes] = source[i, :piece].astype(F32)
-    shares = own_ref[0, piece : piece + 2].astype(F32) + other_ref[0, piece : piece + 2].astype(F32)
-    loss_ref[0, 0] = jnp.sum(shares)
+            out_ref[into, side * lanes : (side + 1) * lanes] = source[i].astype(F32)
 
 
 def input_grad_kernel(
@@ -357,7 +376,7 @@
     slope_ref[...] = grad_ref[...].astype(BF16)
 
 
-def call(kernel, out_shape, *operands, smem=(), smem_out=(), away=(), loose=False, scratch=(), held=()):
+def call(kernel, out_shape, *operands, smem=(), away=(), away_out=(), loose=False, scratch=(), held=()):
     spaces = [pltpu.VMEM for _ in operands]
     for i in smem:
         spaces[i] = pltpu.SMEM
@@ -373,7 +392,9 @@
         shape if loose else (pltpu.VMEM if i in held else pltpu.HBM)(shape.shape, shape.dtype)
         for i, shape in enumerate(out_shape)
     ]
-    out_spaces = [pltpu.SMEM if i in smem_out else pltpu.VMEM for i in range(len(shapes))]
+    out_spaces = [pltpu.VMEM for _ in shapes]
+    for i in away_out:
+        out_spaces[i] = pl.ANY
     return pl.pallas_call(
         kernel,
         out_shape=shapes,
@@ -397,40 +418,35 @@
         mine,
         arrived,
         loss,
-        loose=True,
     )
     summed = lax.all_to_all(summed, "ens", 0, 0, tiled=True)
 
-    def marked(total):
-        share = total[piece : piece + 1] + total[piece + 1 : piece + 2]
-        blank = jnp.zeros((6, lanes), BF16)
-        return jnp.concatenate([total[:piece].astype(BF16), *split(share), blank], 0)
-
     total = jnp.sum(summed.astype(F32), 0)
-    sent = marked(total)
+    share = total[piece : piece + 1] + total[piece + 1 : piece + 2]
+    blank = jnp.zeros((6, lanes), BF16)
+    sent = jnp.concatenate([total[:piece].astype(BF16), *split(share), blank], 0)
     arrived = [
         lax.ppermute(sent, "lat", [(i, (i + step) % lat_count) for i in range(lat_count)])
         for step in range(1, lat_count)
     ]
     for block in arrived:
         total = total + block.astype(F32)
-    spread_out = jnp.broadcast_to(marked(total)[None], summed.shape)
+    spread_out = jnp.broadcast_to(
+        total[None, :piece].astype(BF16), (ens_count, piece, lanes)
+    )
     gathered = lax.all_to_all(spread_out, "ens", 0, 0, tiled=True)
     other = lax.ppermute(gathered, "lon", swap)
-    whole, loss = call(
+    shares = total[piece:]
+    loss = jnp.sum((shares + lax.ppermute(shares, "lon", swap))[:2])
+    (whole,) = call(
         whole_kernel,
-        (
-            jax.ShapeDtypeStruct((rows, 2 * lanes), F32),
-            jax.ShapeDtypeStruct((1, 1), F32),
-        ),
+        (jax.ShapeDtypeStruct((rows, 2 * lanes), F32),),
         gathered,
         other,
         lon_index[None],
         smem=(2,),
-        smem_out=(1,),
-        loose=True,
-    )
-    return whole, loss[0, 0]
+    )
+    return whole, loss
 
 
 def step(inputs, weight, spread, target):
@@ -441,12 +457,35 @@
     lon_total = width * lax.axis_size("lon")
     lat_index, lon_index, ens_index = (lax.axis_index(a) for a in ("lat", "lon", "ens"))
     field = inputs[0]
-    wave_cols, basis = circle_waves(lon_index, width, lon_total)
+    wave_cols, basis, all_basis = circle_waves(lon_index, width, lon_total)
     rows_around = lat_index * row_count - 1 + jnp.arange(row_count + 2)
     polar = (rows_around < PCAP) | (rows_around >= lat_total - PCAP)
     polar_scale = polar.astype(F32)
 
-    own = extend_lon(field, basis, spread, reach)
+    spread_scale = spread.astype(F32)
+    sums, parcel = call(
+        parcel_kernel,
+        (
+            jax.ShapeDtypeStruct((row_count, 3, channels), F32),
+            jax.ShapeDtypeStruct((row_count, 3 * reach, channels), BF16),
+        ),
+        field,
+        all_basis,
+        lon_index[None],
+        smem=(2,),
+        held=(0, 1),
+    )
+    other = lax.ppermute(parcel, "lon", [(0, 1), (1, 0)])
+    (own,) = call(
+        extend_kernel,
+        (jax.ShapeDtypeStruct((row_count, width + 3 * reach, channels), BF16),),
+        field,
+        sums,
+        other,
+        spread_scale,
+        smem=(3,),
+        held=(0,),
+    )
     low, high = lat_neighbours(own)
     own_band = band_blocks(spread, ~polar[1:3], reach)
     own_polar = polar_scale[1:3]
@@ -523,14 +562,16 @@
         wave_cols,
         own_polar,
         lon_index[None],
-        spread.astype(F32),
+        spread_scale,
         smem=(8, 9, 10),
         away=(0, 3, 4, 5),
+        away_out=(0, 1),
         loose=True,
         scratch=[
             pltpu.VMEM((row_count, width, 3 * channels), BF16),
             pltpu.VMEM((row_count + 2, width, channels), BF16),
-            pltpu.SemaphoreType.DMA((6,)),
+            pltpu.VMEM((2, *half.shape), BF16),
+            pltpu.SemaphoreType.DMA((8,)),
         ],
     )
     slope_low, slope_high = lat_neighbours(slope_own)

time: 186 us -> 182 us (0.978)
  waiting for transfers between devices: 59.3 us -> 55.3 us
  starting transfers between devices: 44.7 us -> 47.4 us
  Pallas kernels: 35 us -> 32.4 us
  local copies, waits for them, and re-layouts: 8.84 us -> 11.1 us
    ppermute x0 -> x2, starting transfers between devices: none -> 6.42 us  [the longest x1 3.29 us: step(): other = lax.ppermute(parcel, 'lon', [(0, 1), (1, 0)])]
    all_to_all x1, waiting for transfers between devices: 7.02 us -> 2.59 us  [reduce_weight_grad(): gathered = lax.all_to_all(spread_out, 'ens', 0, 0, tiled=True)]
    ppermute x2 -> x1, starting transfers between devices: 7.57 us -> 4.28 us  [circle_parcel(): return (sums, lax.ppermute(parcel, 'lon', [(0, 1), (1, 0)]))]
    unnamed x38 -> x42, local copies, waits for them, and re-layouts: 2.34 us -> 5.03 us
    pallas_call x7 -> x9, Pallas kernels: 35 us -> 32.4 us  [call(): pl.pallas_call(kernel, out_shape=shapes, in_specs=[pl.BlockSpec(memory_sp...]
  transfers between devices with their start and end apart: 14 -> 15, of which waited for: 9 -> 9; matrix products, arithmetic and copies ran while one was open for 6% -> 7% of each run, Pallas kernels for 6% -> 6%
where the time goes in v2:
time: 182 us; the launch traced here: 181 us
  waiting for transfers between devices  55.3 us (30%)
  starting transfers between devices  47.4 us (26%)
  Pallas kernels  32.4 us (18%)
  blocking collectives  25.4 us (14%)
  local copies, waits for them, and re-layouts  11.1 us (6%)
  other arithmetic  8.03 us (4%)
    pallas_call x9, Pallas kernels, call(): pl.pallas_call(kernel, out_shape=shapes, in_specs=[pl.BlockSpec(memory_sp...  32.4 us
    all_to_all x1, blocking collectives, step(): slopes = lax.all_to_all(slopes, 'ens', 0, 0, tiled=True)  25.4 us
    all_to_all x1, waiting for transfers between devices, step(): lax.all_to_all(sent.reshape(members, cells, channels), 'ens', 0, 0, tiled...  20.9 us
    all_to_all x1, waiting for transfers between devices, reduce_weight_grad(): summed = lax.all_to_all(summed, 'ens', 0, 0, tiled=True)  18.7 us
    all_to_all x1, starting transfers between devices, step(): lax.all_to_all(sent.reshape(members, cells, channels), 'ens', 0, 0, tiled...  11.2 us
    all_to_all x1, starting transfers between devices, reduce_weight_grad(): gathered = lax.all_to_all(spread_out, 'ens', 0, 0, tiled=True)  5.92 us
    ppermute x1, starting transfers between devices, reduce_weight_grad(): other = lax.ppermute(gathered, 'lon', swap)  5.36 us
    unnamed x42, local copies, waits for them, and re-layouts  5.03 us
  transfers between devices with their start and end apart: 15, of which 9 were waited for; matrix products, arithmetic and copies ran while one was open for 7% of the time, Pallas kernels for 6%

profile of v2, /device:TPU:1, one launch (start us, length us, event | category | flops | bytes accessed | tf_op | source)
XLA Modules:
  0.0 181.0 jit_solution(11219206803441778034)
XLA Ops:
  0.7 1.2 copy-done.5
  1.9 0.7 copy-done.10
  2.6 0.2 shard_map.93
  2.8 3.3 %collective-permute-start = (bf16[2,48,256]{2,1,0:T(8,128)(2,1)S(1)}, bf16[2,48,256]{2,1,0:T(8,128)(2,1)S(1)}, u32[]{:S(2)}, u32[]{:S(2)}) collective-permute-start(bf16[2,48,256]{2,1,0:T(8,128)(2,1)S(1)} %get-tuple-element.14), channel_id=1, source_target_pairs={{0,32},{32,0},{1,33},{33,1},{2,34},{34,2},{3,35},{35,3},{4,36},{36... | collective-permute-start | bytes 147464 | tf_op jit(solution)/shard_map/ppermute | solution.py:478
  6.1 0.7 fusion.5
  6.8 0.1 slice_not_fusion
  6.9 0.1 broadcast_multiply_fusion.1
  7.0 1.0 dynamic-slice_bitcast_fusion.wave_ref
  8.0 0.1 slice.72.flag_ref
  8.1 0.6 shard_map.94.own_ref
  8.7 0.1 fusion.10
  8.8 1.6 collective-permute-start.1
  10.4 1.3 collective-permute-start.2
  11.7 0.4 select_convert_fusion.1.band_ref
  12.1 3.6 %shard_map.95.begun_ref = f32[2,720,256]{2,1,0:T(8,128)S(1)} custom-call(bf16[2,768,256]{2,1,0:T(8,128)(2,1)S(1)} %shard_map.94.own_ref, bf16[9,256,256]{2,1,0:T(8,128)(2,1)S(1)} %copy-done.3, bf16[2,3,224,256]{3,2,1,0:T(8,128)(2,1)S(1)} %select_convert_fusion.1.band_ref, f32[720,2]{1,0:T(8,128)S(1)} %dynamic-slice_bitcast_fusion.wave_ref, f32[2]{0:T(128)S(1)} %slice.72.flag_ref), custom_call_target="tpu_custom_call" | custom-call | tf_op jit(solution)/shard_map/pallas_call | solution.py:398
  15.7 3.1 %collective-permute-done.1.low_ref = bf16[1,768,256]{2,1,0:T(8,128)(2,1)S(1)} collective-permute-done((bf16[1,768,256]{2,1,0:T(8,128)(2,1)S(1)}, bf16[1,768,256]{2,1,0:T(8,128)(2,1)S(1)}, u32[]{:S(2)}, u32[]{:S(2)}) %collective-permute-start.1) | collective-permute-done | bytes 393248 | tf_op jit(solution)/shard_map/ppermute | solution.py:106
  18.8 3.9 %collective-permute-done.2.high_ref = bf16[1,768,256]{2,1,0:T(8,128)(2,1)S(1)} collective-permute-done((bf16[1,768,256]{2,1,0:T(8,128)(2,1)S(1)}, bf16[1,768,256]{2,1,0:T(8,128)(2,1)S(1)}, u32[]{:S(2)}, u32[]{:S(2)}) %collective-permute-start.2) | collective-permute-done | bytes 393248 | tf_op jit(solution)/shard_map/ppermute | solution.py:107
  22.7 3.9 %shard_map.96 = (bf16[2,720,256]{2,1,0:T(8,128)(2,1)}, bf16[1536,256]{1,0:T(8,128)(2,1)}) custom-call(bf16[1,768,256]{2,1,0:T(8,128)(2,1)S(1)} %collective-permute-done.1.low_ref, bf16[1,768,256]{2,1,0:T(8,128)(2,1)S(1)} %collective-permute-done.2.high_ref, f32[2,720,256]{2,1,0:T(8,128)S(1)} %shard_map.95.begun_ref, bf16[9,256,256]{2,1,0:T(8,128)(2,1)S(1)} %copy-done.3, ...), custom_call_target="tpu_custom_call" | custom-call | tf_op jit(solution)/shard_map/pallas_call | solution.py:398
  26.6 11.2 %all-to-all-start = ((bf16[32,48,256]{2,1,0:T(8,128)(2,1)}), bf16[32,48,256]{2,1,0:T(8,128)(2,1)S(1)}, u32[]{:S(2)}, u32[]{:S(2)}) async-start(bf16[32,48,256]{2,1,0:T(8,128)(2,1)} %bitcast.30), calls=%async_computation | async-start | bytes 1572864 | tf_op jit(solution)/shard_map/all_to_all | solution.py:519
  37.9 20.9 %all-to-all-done.z_ref = bf16[32,48,256]{2,1,0:T(8,128)(2,1)S(1)} async-done(((bf16[32,48,256]{2,1,0:T(8,128)(2,1)}), bf16[32,48,256]{2,1,0:T(8,128)(2,1)S(1)}, u32[]{:S(2)}, u32[]{:S(2)}) %all-to-all-start) | async-done | bytes 786464 | tf_op jit(solution)/shard_map/all_to_all | solution.py:519
  58.8 7.3 %shard_map.97 = (bf16[32,48,256]{2,1,0:T(8,128)(2,1)S(1)}, f32[8,128]{1,0:T(8,128)S(1)}) custom-call(bf16[32,48,256]{2,1,0:T(8,128)(2,1)S(1)} %all-to-all-done.z_ref, bf16[48,256]{1,0:T(8,128)(2,1)S(1)} %constant_dynamic-slice_fusion.truth_ref, f32[1]{0:T(128)} %bitcast.6.weight_ref), custom_call_target="tpu_custom_call" | custom-call | tf_op jit(solution)/shard_map/pallas_call | solution.py:398
  66.1 25.4 %all_to_all.20 = bf16[32,48,256]{2,1,0:T(8,128)(2,1)S(1)} all-to-all(bf16[32,48,256]{2,1,0:T(8,128)(2,1)S(1)} %get-tuple-element.17), channel_id=1, replica_groups=mesh['lat'=4,'lon'=2,'ens'=32] {'ens'}, dimensions={0} | all-to-all | bytes 1572864 | tf_op jit(solution)/shard_map/all_to_all | solution.py:544
  91.6 0.2 convolution_bitcast_fusion
  91.8 0.6 fusion.2
  92.4 0.2 concatenate.17
  92.6 4.3 %collective-permute-start.3 = (bf16[2,48,256]{2,1,0:T(8,128)(2,1)S(1)}, bf16[2,48,256]{2,1,0:T(8,128)(2,1)S(1)}, u32[]{:S(2)}, u32[]{:S(2)}) collective-permute-start(bf16[2,48,256]{2,1,0:T(8,128)(2,1)S(1)} %concatenate.17), channel_id=1, source_target_pairs={{0,32},{32,0},{1,33},{33,1},{2,34},{34,2},{3,35},{35,3},{4,36},{36... | collective-permute-start | bytes 147464 | tf_op jit(solution)/shard_map/ppermute | solution.py:63
  96.9 0.9 collective-permute-done.3.other_ref
  97.8 0.6 copy-done.18
  98.4 7.3 %shard_map.98 = (bf16[2304,128]{1,0:T(8,128)(2,1)}, bf16[2304,128]{1,0:T(8,128)(2,1)}, bf16[2,768,256]{2,1,0:T(8,128)(2,1)}) custom-call(bf16[1536,256]{1,0:T(8,128)(2,1)} %bitcast.26, f32[2,3,256]{2,1,0:T(4,128)} %get-tuple-element.32.sums_ref, bf16[2,48,256]{2,1,0:T(8,128)(2,1)} %copy-done.18, bf16[1,768,256]{2,1,0:T(8,128)(2,1)} %copy-done.7, ...), custom_call_target="tpu_custom_call" | custom-call | tf_op jit(solution)/shard_map/pallas_call | solution.py:398
  105.7 0.6 collective-permute-start.6
  106.4 1.8 %collective-permute-done.6.theirs_ref = bf16[2304,128]{1,0:T(8,128)(2,1)S(1)} collective-permute-done((bf16[2304,128]{1,0:T(8,128)(2,1)}, bf16[2304,128]{1,0:T(8,128)(2,1)S(1)}, u32[]{:S(2)}, u32[]{:S(2)}) %collective-permute-start.6) | collective-permute-done | bytes 589856 | tf_op jit(solution)/shard_map/ppermute | solution.py:414
  108.2 1.1 copy-done.9
  109.3 1.0 shard_map.100
  110.2 4.7 %all-to-all-start.2 = ((bf16[32,80,128]{2,1,0:T(8,128)(2,1)}), bf16[32,80,128]{2,1,0:T(8,128)(2,1)S(1)}, u32[]{:S(2)}, u32[]{:S(2)}) async-start(bf16[32,80,128]{2,1,0:T(8,128)(2,1)} %shard_map.100), calls=%async_computation.2 | async-start | bytes 1310720 | tf_op jit(solution)/shard_map/all_to_all | solution.py:422
  115.0 0.1 pad.3.clone
  115.1 18.7 %all-to-all-done.2 = bf16[32,80,128]{2,1,0:T(8,128)(2,1)S(1)} async-done(((bf16[32,80,128]{2,1,0:T(8,128)(2,1)}), bf16[32,80,128]{2,1,0:T(8,128)(2,1)S(1)}, u32[]{:S(2)}, u32[]{:S(2)}) %all-to-all-start.2) | async-done | bytes 655392 | tf_op jit(solution)/shard_map/all_to_all | solution.py:422
  133.8 0.1 convert_reduce_fusion
  133.9 0.1 maximum_maximum_fusion
  134.0 0.6 collective-permute-start.9
  134.6 2.5 %collective-permute-start.8 = (bf16[80,128]{1,0:T(8,128)(2,1)S(1)}, bf16[80,128]{1,0:T(8,128)(2,1)S(1)}, u32[]{:S(2)}, u32[]{:S(2)}) collective-permute-start(bf16[80,128]{1,0:T(8,128)(2,1)S(1)} %maximum_maximum_fusion), channel_id=1, source_target_pairs={{0,128},{64,192},{128,0},{192,64},{1,129},{65,193},{129,1},{193,65... | collective-permute-start | bytes 61448 | tf_op jit(solution)/shard_map/ppermute | solution.py:429
  137.0 0.3 collective-permute-start.7
  137.4 1.3 collective-permute-done.8
  138.7 2.2 %collective-permute-done.7 = bf16[80,128]{1,0:T(8,128)(2,1)S(1)} collective-permute-done((bf16[80,128]{1,0:T(8,128)(2,1)S(1)}, bf16[80,128]{1,0:T(8,128)(2,1)S(1)}, u32[]{:S(2)}, u32[]{:S(2)}) %collective-permute-start.7) | collective-permute-done | bytes 20512 | tf_op jit(solution)/shard_map/ppermute | solution.py:429
  140.9 0.6 copy-done.17
  141.5 0.9 broadcast_in_dim.83
  142.4 5.9 %all-to-all-start.3 = ((bf16[32,72,128]{2,1,0:T(8,128)(2,1)}), bf16[32,72,128]{2,1,0:T(8,128)(2,1)S(1)}, u32[]{:S(2)}, u32[]{:S(2)}) async-start(bf16[32,72,128]{2,1,0:T(8,128)(2,1)} %broadcast_in_dim.83), calls=%async_computation.3 | async-start | bytes 1179648 | tf_op jit(solution)/shard_map/all_to_all | solution.py:437
  148.4 1.2 slice.100
  149.6 1.2 slice.99
  150.7 1.4 maximum_convert_fusion
  152.1 0.6 fusion.12
  152.7 1.4 fusion.6
  154.1 0.1 broadcast_multiply_fusion
  154.2 1.3 collective-permute-start.4
  155.5 1.3 collective-permute-start.5
  156.8 0.7 slice.105
  157.5 3.1 %collective-permute-start.11 = (f32[8,128]{1,0:T(8,128)S(1)}, f32[8,128]{1,0:T(8,128)S(1)}, u32[]{:S(2)}, u32[]{:S(2)}) collective-permute-start(f32[8,128]{1,0:T(8,128)S(1)} %slice.105), channel_id=1, source_target_pairs={{0,32},{32,0},{1,33},{33,1},{2,34},{34,2},{3,35},{35,3},{4,36},{36... | collective-permute-start | bytes 12296 | tf_op jit(solution)/shard_map/ppermute | solution.py:440
  160.6 2.6 %all-to-all-done.3.own_ref = bf16[32,72,128]{2,1,0:T(8,128)(2,1)S(1)} async-done(((bf16[32,72,128]{2,1,0:T(8,128)(2,1)}), bf16[32,72,128]{2,1,0:T(8,128)(2,1)S(1)}, u32[]{:S(2)}, u32[]{:S(2)}) %all-to-all-start.3) | async-done | bytes 589856 | tf_op jit(solution)/shard_map/all_to_all | solution.py:437
  163.2 5.4 %collective-permute-start.10 = (bf16[32,72,128]{2,1,0:T(8,128)(2,1)S(1)}, bf16[32,72,128]{2,1,0:T(8,128)(2,1)S(1)}, u32[]{:S(2)}, u32[]{:S(2)}) collective-permute-start(bf16[32,72,128]{2,1,0:T(8,128)(2,1)S(1)} %all-to-all-done.3.own_ref), channel_id=1, source_target_pairs={{0,32},{32,0},{1,33},{33,1},{2,34},{34,2},{3,35},{35,3},{4,36},{36... | collective-permute-start | bytes 1769480 | tf_op jit(solution)/shard_map/ppermute | solution.py:438
  168.6 1.8 %select_convert_fusion.band_ref = bf16[4,3,224,256]{3,2,1,0:T(8,128)(2,1)} fusion(f32[4]{0:T(128)S(1)} %fusion.6, f32[4,3]{1,0:T(4,128)S(1)} %broadcast_multiply_fusion, f32[224,256]{1,0:T(8,128)S(1)} %subtract_convert_fusion, pred[4]{0:T(512)(128)(4,1)S(1)} %fusion.7), kind=kLoop, calls=%fused_computation | loop fusion | flops 5505024 | bytes 1605700 | tf_op jit(solution)/shard_map/convert_element_type | solution.py:53
  170.4 0.8 copy-done.16
  171.2 7.0 %shard_map.99 = bf16[2,720,256]{2,1,0:T(8,128)(2,1)} custom-call(bf16[1,768,256]{2,1,0:T(8,128)(2,1)} %copy-done.16, bf16[2,768,256]{2,1,0:T(8,128)(2,1)} %get-tuple-element.18.own_ref, bf16[1,768,256]{2,1,0:T(8,128)(2,1)} %collective-permute-done.5.high_ref, bf16[9,256,256]{2,1,0:T(8,128)(2,1)} %weight_ref.5, ...), custom_call_target="tpu_custom_call" | custom-call | tf_op jit(solution)/shard_map/pallas_call | solution.py:398
  178.1 0.7 slice_add_fusion.2
  178.8 0.6 slice_reduce_fusion
  179.4 1.6 shard_map.101
  (63 shorter events, 0.4 us)
Async XLA Ops:
  0.6 37.3 %copy-start = (bf16[2,720,256]{2,1,0:T(8,128)(2,1)S(1)}, bf16[2,720,256]{2,1,0:T(8,128)(2,1)}, u32[]{:S(2)}) copy-start(bf16[2,720,256]{2,1,0:T(8,128)(2,1)} %param.9) | copy-start | bytes 2211844
  0.6 7.4 %copy-start.19 = (s32[2]{0:T(128)S(1)}, s32[2]{0:T(128)}, u32[]{:S(2)}) copy-start(s32[2]{0:T(128)} %param.8) | copy-start | bytes 28
  0.7 1.2 copy-start.5
  1.8 0.7 copy-start.10
  2.6 5.5 %copy-start.6 = (bf16[1,2,720,256]{3,2,1,0:T(8,128)(2,1)S(1)}, bf16[1,2,720,256]{3,2,1,0:T(8,128)(2,1)}, u32[]{:S(2)}) copy-start(bf16[1,2,720,256]{3,2,1,0:T(8,128)(2,1)} %param.6) | copy-start | bytes 2211844
  2.8 5.3 %collective-permute-start = (bf16[2,48,256]{2,1,0:T(8,128)(2,1)S(1)}, bf16[2,48,256]{2,1,0:T(8,128)(2,1)S(1)}, u32[]{:S(2)}, u32[]{:S(2)}) collective-permute-start(bf16[2,48,256]{2,1,0:T(8,128)(2,1)S(1)} %get-tuple-element.14), channel_id=1, source_target_pairs={{0,32},{32,0},{1,33},{33,1},{2,34},{34,2},{3,35},{35,3},{4,36},{36... | collective-permute-start | bytes 147464 | tf_op jit(solution)/shard_map/ppermute | solution.py:478
  8.0 14.7 %copy-start.4 = (f32[720,2]{1,0:T(8,128)}, f32[720,2]{1,0:T(8,128)S(1)}, u32[]{:S(2)}) copy-start(f32[720,2]{1,0:T(8,128)S(1)} %dynamic-slice_bitcast_fusion.wave_ref) | copy-start | bytes 17284
  8.0 0.8 copy-start.20
  8.0 0.8 copy-start.13
  8.1 14.5 %copy-start.12 = (f32[2]{0:T(128)}, f32[2]{0:T(128)S(1)}, u32[]{:S(2)}) copy-start(f32[2]{0:T(128)S(1)} %slice.72.flag_ref) | copy-start | bytes 28
  8.7 7.0 %copy-start.1 = (bf16[2,768,256]{2,1,0:T(8,128)(2,1)}, bf16[2,768,256]{2,1,0:T(8,128)(2,1)S(1)}, u32[]{:S(2)}) copy-start(bf16[2,768,256]{2,1,0:T(8,128)(2,1)S(1)} %shard_map.94.own_ref) | copy-start | bytes 2359300
  8.7 3.4 %copy-start.3 = (bf16[9,256,256]{2,1,0:T(8,128)(2,1)S(1)}, bf16[9,256,256]{2,1,0:T(8,128)(2,1)}, u32[]{:S(2)}) copy-start(bf16[9,256,256]{2,1,0:T(8,128)(2,1)} %weight_ref.5) | copy-start | bytes 3538948
  8.8 10.0 %collective-permute-start.1 = (bf16[1,768,256]{2,1,0:T(8,128)(2,1)S(1)}, bf16[1,768,256]{2,1,0:T(8,128)(2,1)S(1)}, u32[]{:S(2)}, u32[]{:S(2)}) collective-permute-start(bf16[1,768,256]{2,1,0:T(8,128)(2,1)S(1)} %get-tuple-element.25), channel_id=1, source_target_pairs={{0,64},{64,128},{128,192},{1,65},{65,129},{129,193},{2,66},{66,130... | collective-permute-start | bytes 1179656 | tf_op jit(solution)/shard_map/ppermute | solution.py:106
  10.4 12.3 %collective-permute-start.2 = (bf16[1,768,256]{2,1,0:T(8,128)(2,1)S(1)}, bf16[1,768,256]{2,1,0:T(8,128)(2,1)S(1)}, u32[]{:S(2)}, u32[]{:S(2)}) collective-permute-start(bf16[1,768,256]{2,1,0:T(8,128)(2,1)S(1)} %get-tuple-element.24), channel_id=1, source_target_pairs={{64,0},{128,64},{192,128},{65,1},{129,65},{193,129},{66,2},{130,66... | collective-permute-start | bytes 1179656 | tf_op jit(solution)/shard_map/ppermute | solution.py:107
  12.1 10.5 %copy-start.2 = (bf16[2,3,224,256]{3,2,1,0:T(8,128)(2,1)}, bf16[2,3,224,256]{3,2,1,0:T(8,128)(2,1)S(1)}, u32[]{:S(2)}) copy-start(bf16[2,3,224,256]{3,2,1,0:T(8,128)(2,1)S(1)} %select_convert_fusion.1.band_ref) | copy-start | bytes 2064388
  18.8 7.8 %copy-start.7 = (bf16[1,768,256]{2,1,0:T(8,128)(2,1)}, bf16[1,768,256]{2,1,0:T(8,128)(2,1)S(1)}, u32[]{:S(2)}) copy-start(bf16[1,768,256]{2,1,0:T(8,128)(2,1)S(1)} %collective-permute-done.1.low_ref) | copy-start | bytes 1179652
  22.7 3.9 %copy-start.8 = (bf16[1,768,256]{2,1,0:T(8,128)(2,1)}, bf16[1,768,256]{2,1,0:T(8,128)(2,1)S(1)}, u32[]{:S(2)}) copy-start(bf16[1,768,256]{2,1,0:T(8,128)(2,1)S(1)} %collective-permute-done.2.high_ref) | copy-start | bytes 1179652
  26.6 32.2 %all-to-all-start = ((bf16[32,48,256]{2,1,0:T(8,128)(2,1)}), bf16[32,48,256]{2,1,0:T(8,128)(2,1)S(1)}, u32[]{:S(2)}, u32[]{:S(2)}) async-start(bf16[32,48,256]{2,1,0:T(8,128)(2,1)} %bitcast.30), calls=%async_computation | async-start | bytes 1572864 | tf_op jit(solution)/shard_map/all_to_all | solution.py:519
  66.1 25.5 %copy-start.11 = (bf16[2,5,720]{2,1,0:T(8,128)(2,1)S(1)}, bf16[2,5,720]{2,1,0:T(8,128)(2,1)}, u32[]{:S(2)}) copy-start(bf16[2,5,720]{2,1,0:T(8,128)(2,1)} %constant.87.clone.basis_ref) | copy-start | bytes 43204
  91.5 6.2 %copy-start.14 = (bf16[32,48,256]{2,1,0:T(8,128)(2,1)}, bf16[32,48,256]{2,1,0:T(8,128)(2,1)S(1)}, u32[]{:S(2)}) copy-start(bf16[32,48,256]{2,1,0:T(8,128)(2,1)S(1)} %all_to_all.20) | copy-start | bytes 2359300
  92.6 5.2 %collective-permute-start.3 = (bf16[2,48,256]{2,1,0:T(8,128)(2,1)S(1)}, bf16[2,48,256]{2,1,0:T(8,128)(2,1)S(1)}, u32[]{:S(2)}, u32[]{:S(2)}) collective-permute-start(bf16[2,48,256]{2,1,0:T(8,128)(2,1)S(1)} %concatenate.17), channel_id=1, source_target_pairs={{0,32},{32,0},{1,33},{33,1},{2,34},{34,2},{3,35},{35,3},{4,36},{36... | collective-permute-start | bytes 147464 | tf_op jit(solution)/shard_map/ppermute | solution.py:63
  97.8 0.6 copy-start.18
  105.7 2.5 %collective-permute-start.6 = (bf16[2304,128]{1,0:T(8,128)(2,1)}, bf16[2304,128]{1,0:T(8,128)(2,1)S(1)}, u32[]{:S(2)}, u32[]{:S(2)}) collective-permute-start(bf16[2304,128]{1,0:T(8,128)(2,1)} %get-tuple-element.20), channel_id=1, source_target_pairs={{0,32},{32,0},{1,33},{33,1},{2,34},{34,2},{3,35},{35,3},{4,36},{36... | collective-permute-start | bytes 1769480 | tf_op jit(solution)/shard_map/ppermute | solution.py:414
  108.2 1.1 copy-start.9
  110.2 23.6 %all-to-all-start.2 = ((bf16[32,80,128]{2,1,0:T(8,128)(2,1)}), bf16[32,80,128]{2,1,0:T(8,128)(2,1)S(1)}, u32[]{:S(2)}, u32[]{:S(2)}) async-start(bf16[32,80,128]{2,1,0:T(8,128)(2,1)} %shard_map.100), calls=%async_computation.2 | async-start | bytes 1310720 | tf_op jit(solution)/shard_map/all_to_all | solution.py:422
  115.1 39.0 %copy-start.15 = (bf16[2,768,256]{2,1,0:T(8,128)(2,1)S(1)}, bf16[2,768,256]{2,1,0:T(8,128)(2,1)}, u32[]{:S(2)}) copy-start(bf16[2,768,256]{2,1,0:T(8,128)(2,1)} %get-tuple-element.18.own_ref) | copy-start | bytes 2359300
  134.0 3.4 %collective-permute-start.9 = (bf16[80,128]{1,0:T(8,128)(2,1)S(1)}, bf16[80,128]{1,0:T(8,128)(2,1)S(1)}, u32[]{:S(2)}, u32[]{:S(2)}) collective-permute-start(bf16[80,128]{1,0:T(8,128)(2,1)S(1)} %maximum_maximum_fusion), channel_id=1, source_target_pairs={{0,192},{64,0},{128,64},{192,128},{1,193},{65,1},{129,65},{193,129... | collective-permute-start | bytes 61448 | tf_op jit(solution)/shard_map/ppermute | solution.py:429
  134.6 4.1 %collective-permute-start.8 = (bf16[80,128]{1,0:T(8,128)(2,1)S(1)}, bf16[80,128]{1,0:T(8,128)(2,1)S(1)}, u32[]{:S(2)}, u32[]{:S(2)}) collective-permute-start(bf16[80,128]{1,0:T(8,128)(2,1)S(1)} %maximum_maximum_fusion), channel_id=1, source_target_pairs={{0,128},{64,192},{128,0},{192,64},{1,129},{65,193},{129,1},{193,65... | collective-permute-start | bytes 61448 | tf_op jit(solution)/shard_map/ppermute | solution.py:429
  137.0 3.8 %collective-permute-start.7 = (bf16[80,128]{1,0:T(8,128)(2,1)S(1)}, bf16[80,128]{1,0:T(8,128)(2,1)S(1)}, u32[]{:S(2)}, u32[]{:S(2)}) collective-permute-start(bf16[80,128]{1,0:T(8,128)(2,1)S(1)} %maximum_maximum_fusion), channel_id=1, source_target_pairs={{0,64},{64,128},{128,192},{192,0},{1,65},{65,129},{129,193},{193,1... | collective-permute-start | bytes 61448 | tf_op jit(solution)/shard_map/ppermute | solution.py:429
  140.9 0.6 copy-start.17
  142.4 20.8 %all-to-all-start.3 = ((bf16[32,72,128]{2,1,0:T(8,128)(2,1)}), bf16[32,72,128]{2,1,0:T(8,128)(2,1)S(1)}, u32[]{:S(2)}, u32[]{:S(2)}) async-start(bf16[32,72,128]{2,1,0:T(8,128)(2,1)} %broadcast_in_dim.83), calls=%async_computation.3 | async-start | bytes 1179648 | tf_op jit(solution)/shard_map/all_to_all | solution.py:437
  154.2 16.2 %collective-permute-start.4 = (bf16[1,768,256]{2,1,0:T(8,128)(2,1)S(1)}, bf16[1,768,256]{2,1,0:T(8,128)(2,1)S(1)}, u32[]{:S(2)}, u32[]{:S(2)}) collective-permute-start(bf16[1,768,256]{2,1,0:T(8,128)(2,1)S(1)} %get-tuple-element.23), channel_id=1, source_target_pairs={{0,64},{64,128},{128,192},{1,65},{65,129},{129,193},{2,66},{66,130... | collective-permute-start | bytes 1179656 | tf_op jit(solution)/shard_map/ppermute | solution.py:106
  155.5 14.9 %collective-permute-start.5 = (bf16[1,768,256]{2,1,0:T(8,128)(2,1)S(1)}, bf16[1,768,256]{2,1,0:T(8,128)(2,1)}, u32[]{:S(2)}, u32[]{:S(2)}) collective-permute-start(bf16[1,768,256]{2,1,0:T(8,128)(2,1)S(1)} %get-tuple-element.22), channel_id=1, source_target_pairs={{64,0},{128,64},{192,128},{65,1},{129,65},{193,129},{66,2},{130,66... | collective-permute-start | bytes 1179656 | tf_op jit(solution)/shard_map/ppermute | solution.py:107
  157.5 20.6 %collective-permute-start.11 = (f32[8,128]{1,0:T(8,128)S(1)}, f32[8,128]{1,0:T(8,128)S(1)}, u32[]{:S(2)}, u32[]{:S(2)}) collective-permute-start(f32[8,128]{1,0:T(8,128)S(1)} %slice.105), channel_id=1, source_target_pairs={{0,32},{32,0},{1,33},{33,1},{2,34},{34,2},{3,35},{35,3},{4,36},{36... | collective-permute-start | bytes 12296 | tf_op jit(solution)/shard_map/ppermute | solution.py:440
  163.2 16.2 %collective-permute-start.10 = (bf16[32,72,128]{2,1,0:T(8,128)(2,1)S(1)}, bf16[32,72,128]{2,1,0:T(8,128)(2,1)S(1)}, u32[]{:S(2)}, u32[]{:S(2)}) collective-permute-start(bf16[32,72,128]{2,1,0:T(8,128)(2,1)S(1)} %all-to-all-done.3.own_ref), channel_id=1, source_target_pairs={{0,32},{32,0},{1,33},{33,1},{2,34},{34,2},{3,35},{35,3},{4,36},{36... | collective-permute-start | bytes 1769480 | tf_op jit(solution)/shard_map/ppermute | solution.py:438
  170.4 0.8 copy-start.16
